TPU v7x, 256 devices: a whole 4x4x8 slice. The times are simulated.
256 devices in a mesh: samp: 32 (over z, x_hi, core), var: 8 (over x_lo, y).
Axes of the slice: x: 4 (x_hi: 2, x_lo: 2; x = x_hi * 2 + x_lo), y: 4, z: 8, core: 2. Of those that a mesh axis runs over, the one named last changes fastest.
Arguments:
- genotypes: bfloat16 [34560, 32768], P('samp', 'var'), may hold values from 0 to 2, as said below
- residual: float32 [34560, 256], P('samp'), may hold values from -6 to 6
- coefficients: float32 [256, 32768], P('samp', 'var'), may hold values from -0.06 to 0.06
- penalty: float32 [32768], P('var'), may hold values from 0.2 to 3
- colors: int32 [2, 8], P(None, 'var'), may hold values from 0 to 1
Outputs:
- coefficients_out: float32 [256, 32768], P('samp', 'var')
- residual_out: float32 [34560, 256], P('samp')
Inputs may be any that keep to these rules, and one draw needn't show every extreme that they name: `genotypes`: dosages of a genotype, whole numbers. `colors`: entry (r, v) names which of the 2 blocks of group v is updated in round r.
All inputs are finite; a program needn't handle non-finite values.
Results may differ from a plain program's by a relative error of at most 0.014.
Values may be sent and summed in bfloat16 or wider, within the bound.
A program may use at most 64 MiB of HBM per device.

v0:
```python
import jax
import jax.numpy as jnp
from jax import lax
from jax.sharding import PartitionSpec as P

K = 256
BS = 2048
ROUNDS = 2


def from_everyone(array, axis):
    size = lax.axis_size(axis)
    return lax.all_to_all(
        jnp.broadcast_to(array[None], (size, *array.shape)), axis, 0, 0, tiled=True
    )


def of_everyone(array, axis):
    everything = from_everyone(array, axis)
    return jnp.sum(everything.astype(jnp.float32), axis=0)


def cut_along(array, dim, size):
    before, after = (array.shape[:dim], array.shape[dim + 1 :])
    return jnp.moveaxis(array.reshape(*before, size, -1, *after), dim, 0)


def summed_on_arrival(array, axis, dim):
    blocks = cut_along(array, dim, lax.axis_size(axis))
    arrived = lax.all_to_all(blocks, axis, split_axis=0, concat_axis=0, tiled=True)
    return arrived.sum(axis=0)


def over_copies(array, axis):
    return from_everyone(array, axis).sum(axis=0)


def in_order(blocks, dim):
    dims = list(blocks.shape[1:])
    dims[dim] *= blocks.shape[0]
    return jnp.moveaxis(blocks, 0, dim).reshape(dims)


def gathered_copies(array, axis, dim):
    return in_order(from_everyone(array, axis), dim)


def column_moments(block_values):
    wide = block_values.astype(jnp.float32)
    counts = jnp.sum(wide, axis=0)
    squares = jnp.sum(wide * wide, axis=0)
    return (counts, squares)


def shards(genotypes, residual, coefficients, penalty, colors):
    sample_total = genotypes.shape[0] * lax.axis_size("samp")
    local_counts, local_squares = column_moments(genotypes)
    all_counts, all_squares = (
        of_everyone(local_counts.astype(jnp.bfloat16), "samp").astype(jnp.float32),
        of_everyone(local_squares.astype(jnp.bfloat16), "samp").astype(jnp.float32),
    )
    for round_index in range(ROUNDS):
        first_column = colors[round_index, 0] * BS
        block_values = lax.dynamic_slice_in_dim(genotypes, first_column, BS, 1)
        counts = lax.dynamic_slice_in_dim(all_counts, first_column, BS, 0)
        squares = lax.dynamic_slice_in_dim(all_squares, first_column, BS, 0)
        column_mean = counts / sample_total
        column_scale = squares - counts * column_mean
        centered = (block_values.astype(jnp.float32) - column_mean[None, :]).astype(jnp.bfloat16)
        rounded = residual.astype(jnp.bfloat16)
        penalty_part = lax.dynamic_slice_in_dim(penalty, first_column, BS, 0)
        gradient = summed_on_arrival(
            lax.dot_general(
                rounded, centered, (((0,), (0,)), ((), ())), preferred_element_type=jnp.float32
            ),
            "samp",
            0,
        )
        old_rows = lax.dynamic_slice_in_dim(coefficients, first_column, BS, 1)
        shifted = old_rows + gradient / column_scale[None, :]
        norm_total = over_copies(jnp.sum(shifted * shifted, axis=0), "samp")
        group_norm = jnp.sqrt(norm_total + 1e-06)
        shrink = jnp.maximum(0.0, 1.0 - penalty_part * jnp.sqrt(K / column_scale) / group_norm)
        new_rows = shrink[None, :] * shifted
        coefficients = lax.dynamic_update_slice(
            coefficients, new_rows, (jnp.int32(0), first_column)
        )
        own_change = (new_rows - old_rows).astype(jnp.bfloat16)
        change_rows = gathered_copies(own_change, "samp", 0)
        local_correction = lax.dot_general(
            centered, change_rows, (((1,), (1,)), ((), ())), preferred_element_type=jnp.float32
        )
        correction = lax.psum(local_correction, "var")
        residual = residual - correction
    return (coefficients, residual)


def solution(mesh):
    placed = (P("samp", "var"), P("samp", None), P("samp", "var"), P("var"), P(None, "var"))
    return jax.shard_map(
        shards,
        mesh=mesh,
        in_specs=placed,
        out_specs=(P("samp", "var"), P("samp", None)),
        check_vma=False,
    )
```

profile of v0, /device:TPU:1, one launch (start us, length us, event | category | flops | bytes accessed | tf_op | source)
XLA Modules:
  0.0 459.7 jit_solution(15444391986847450979)
XLA Ops:
  7.2 0.9 copy.24
  8.1 5.3 %multiply_reduce_fusion = bf16[4096]{0:T(1024)(128)(2,1)S(1)} fusion(bf16[1080,4096]{1,0:T(8,128)(2,1)} %param.5), kind=kLoop, calls=%fused_computation | loop fusion | flops 13266944 | bytes 8855552 | tf_op jit(solution)/shard_map/reduce_sum | solution.py:51
  14.4 2.2 reduce.5
  16.5 0.9 reshape.63
  17.4 12.6 %all-to-all-start = ((bf16[32,2,2048]{2,1,0:T(2,128)(2,1)}), bf16[32,2,2048]{2,1,0:T(2,128)(2,1)S(1)}, u32[]{:S(2)}, u32[]{:S(2)}) async-start(bf16[32,2,2048]{2,1,0:T(2,128)(2,1)} %reshape.63), calls=%async_computation | async-start | bytes 524288 | tf_op jit(solution)/shard_map/all_to_all | solution.py:13
  30.0 4.8 %reduce_sum.95 = bf16[4096]{0:T(1024)(128)(2,1)S(1)} reduce(bf16[1080,4096]{1,0:T(8,128)(2,1)} %param.5, bf16[]{:T(256)} %constant.20.clone.1), dimensions={0}, to_apply=%region_2.0 | reduce | flops 4419584 | bytes 8855554 | tf_op jit(solution)/shard_map/reduce_sum | solution.py:50
  35.3 2.2 reduce.6
  38.4 4.6 all-to-all-done
  42.9 5.2 %all-to-all-start.1 = ((bf16[32,2,2048]{2,1,0:T(2,128)(2,1)}), bf16[32,2,2048]{2,1,0:T(2,128)(2,1)S(1)}, u32[]{:S(2)}, u32[]{:S(2)}) async-start(bf16[32,2,2048]{2,1,0:T(2,128)(2,1)} %reshape.61), calls=%async_computation.1 | async-start | bytes 524288 | tf_op jit(solution)/shard_map/all_to_all | solution.py:13
  50.7 10.4 %all-to-all-done.1 = bf16[32,2,2048]{2,1,0:T(2,128)(2,1)S(1)} async-done(((bf16[32,2,2048]{2,1,0:T(2,128)(2,1)}), bf16[32,2,2048]{2,1,0:T(2,128)(2,1)S(1)}, u32[]{:S(2)}, u32[]{:S(2)}) %all-to-all-start.1) | async-done | bytes 262176 | tf_op jit(solution)/shard_map/all_to_all | solution.py:13
  61.7 3.8 fusion.5
  65.6 54.5 %all_to_all.49 = f32[32,8,2048]{2,1,0:T(8,128)S(1)} all-to-all(f32[32,8,2048]{2,1,0:T(8,128)S(1)} %fusion.5), channel_id=1, replica_groups=mesh['samp'=32,'var'=8] {'samp'}, dimensions={0} | all-to-all | bytes 4194304 | tf_op jit(solution)/shard_map/all_to_all | solution.py:30
  120.4 18.5 %all_to_all.44 = f32[32,1,2048]{2,1,0:T(1,128)S(1)} all-to-all(f32[32,1,2048]{2,1,0:T(1,128)S(1)} %broadcast_in_dim.14), channel_id=1, replica_groups=mesh['samp'=32,'var'=8] {'samp'}, dimensions={0} | all-to-all | bytes 524288 | tf_op jit(solution)/shard_map/all_to_all | solution.py:13
  139.3 32.1 %all_to_all.45 = bf16[32,8,2048]{2,1,0:T(8,128)(2,1)S(1)} all-to-all(bf16[32,8,2048]{2,1,0:T(8,128)(2,1)S(1)} %broadcast_in_dim.15), channel_id=1, replica_groups=mesh['samp'=32,'var'=8] {'samp'}, dimensions={0} | all-to-all | bytes 2097152 | tf_op jit(solution)/shard_map/all_to_all | solution.py:13
  171.4 4.7 %fusion = f32[1080,256]{1,0:T(8,128)} fusion(f32[2048]{0:T(1024)S(1)} %get-tuple-element.12, bf16[1080,4096]{1,0:T(8,128)(2,1)} %param.5, s32[]{:T(128)S(6)} %select_n.4, bf16[32,8,2048]{2,1,0:T(8,128)(2,1)S(1)} %all_to_all.45), kind=kOutput, calls=%fused_computation.3 | convolution fusion | flops 1139097600 | bytes 6586372 | tf_op jit(solution)/shard_map/dot_general | solution.py:90
  176.2 74.6 %all-reduce.3.cloned.1.call-done = f32[1080,256]{1,0:T(8,128)} async-done(((f32[1080,256]{1,0:T(8,128)}), f32[1080,256]{1,0:T(8,128)}) %all-reduce.3.cloned.1.call-update) | async-done | bytes 1105936 | tf_op jit(solution)/shard_map/psum | solution.py:93
  250.8 1.4 sub.46
  252.2 3.8 fusion.4
  256.0 65.4 %all_to_all.46 = f32[32,8,2048]{2,1,0:T(8,128)S(1)} all-to-all(f32[32,8,2048]{2,1,0:T(8,128)S(1)} %fusion.4), channel_id=1, replica_groups=mesh['samp'=32,'var'=8] {'samp'}, dimensions={0} | all-to-all | bytes 4194304 | tf_op jit(solution)/shard_map/all_to_all | solution.py:30
  321.7 18.5 %all_to_all.47 = f32[32,1,2048]{2,1,0:T(1,128)S(1)} all-to-all(f32[32,1,2048]{2,1,0:T(1,128)S(1)} %broadcast_in_dim.16), channel_id=1, replica_groups=mesh['samp'=32,'var'=8] {'samp'}, dimensions={0} | all-to-all | bytes 524288 | tf_op jit(solution)/shard_map/all_to_all | solution.py:13
  340.6 32.1 %all_to_all.48 = bf16[32,8,2048]{2,1,0:T(8,128)(2,1)S(1)} all-to-all(bf16[32,8,2048]{2,1,0:T(8,128)(2,1)S(1)} %broadcast_in_dim.17), channel_id=1, replica_groups=mesh['samp'=32,'var'=8] {'samp'}, dimensions={0} | all-to-all | bytes 2097152 | tf_op jit(solution)/shard_map/all_to_all | solution.py:13
  372.7 4.6 %fusion.2 = f32[1080,256]{1,0:T(8,128)} fusion(f32[2048]{0:T(1024)S(1)} %get-tuple-element.13, bf16[1080,4096]{1,0:T(8,128)(2,1)} %param.5, s32[]{:T(128)S(6)} %select_n.5, bf16[32,8,2048]{2,1,0:T(8,128)(2,1)S(1)} %all_to_all.48), kind=kOutput, calls=%fused_computation.5 | convolution fusion | flops 1139097600 | bytes 6586372 | tf_op jit(solution)/shard_map/dot_general | solution.py:90
  377.3 73.1 %all-reduce.5.cloned.1.call-done = f32[1080,256]{1,0:T(8,128)} async-done(((f32[1080,256]{1,0:T(8,128)}), f32[1080,256]{1,0:T(8,128)}) %all-reduce.5.cloned.1.call-update) | async-done | bytes 1105936 | tf_op jit(solution)/shard_map/psum | solution.py:93
  450.5 2.4 sub.51
  (38 shorter events, 5.4 us)
Async XLA Ops:
  17.4 25.5 %all-to-all-start = ((bf16[32,2,2048]{2,1,0:T(2,128)(2,1)}), bf16[32,2,2048]{2,1,0:T(2,128)(2,1)S(1)}, u32[]{:S(2)}, u32[]{:S(2)}) async-start(bf16[32,2,2048]{2,1,0:T(2,128)(2,1)} %reshape.63), calls=%async_computation | async-start | bytes 524288 | tf_op jit(solution)/shard_map/all_to_all | solution.py:13
  30.0 18.2 %copy-start.4 = (s32[2,1]{0,1:T(1,128)S(1)}, s32[2,1]{0,1:T(1,128)}, u32[]{:S(2)}) copy-start(s32[2,1]{0,1:T(1,128)} %param.9) | copy-start | bytes 28
  34.8 26.9 %copy-start.1 = (f32[1080,256]{1,0:T(8,128)S(1)}, f32[1080,256]{1,0:T(8,128)}, u32[]{:S(2)}) copy-start(f32[1080,256]{1,0:T(8,128)} %param.6) | copy-start | bytes 3317764
  42.9 18.2 %all-to-all-start.1 = ((bf16[32,2,2048]{2,1,0:T(2,128)(2,1)}), bf16[32,2,2048]{2,1,0:T(2,128)(2,1)S(1)}, u32[]{:S(2)}, u32[]{:S(2)}) async-start(bf16[32,2,2048]{2,1,0:T(2,128)(2,1)} %reshape.61), calls=%async_computation.1 | async-start | bytes 524288 | tf_op jit(solution)/shard_map/all_to_all | solution.py:13
  48.2 202.7 %all-reduce.3.cloned.1.call-start = ((), (), s32[]{:S(2)}) async-start(), calls=%async_computation.8 | async-start | bytes 2211840 | tf_op jit(solution)/shard_map/psum | solution.py:93
  65.6 73.5 %copy-start.3 = (f32[4096]{0:T(1024)S(1)}, f32[4096]{0:T(1024)}, u32[]{:S(2)}) copy-start(f32[4096]{0:T(1024)} %param.8) | copy-start | bytes 49156
  171.4 79.5 %copy-start.2 = (f32[1080,256]{1,0:T(8,128)S(1)}, f32[1080,256]{1,0:T(8,128)}, u32[]{:S(2)}) copy-start(f32[1080,256]{1,0:T(8,128)} %param.6) | copy-start | bytes 3317764
  176.1 274.3 %all-reduce.5.cloned.1.call-start = ((), (), s32[]{:S(2)}) async-start(), calls=%async_computation.9 | async-start | bytes 2211840 | tf_op jit(solution)/shard_map/psum | solution.py:93
  340.5 36.8 %copy-start = (f32[8,4096]{1,0:T(8,128)}, f32[8,4096]{1,0:T(8,128)S(1)}, u32[]{:S(2)}) copy-start(f32[8,4096]{1,0:T(8,128)S(1)} %get-tuple-element.7) | copy-start | bytes 393220
Sparse Core Ops, SparseCore 0:
  176.2 74.5 all-reduce.2
  377.5 72.9 all-reduce.4
where the time goes:
time: 464 us; the launch traced here: 460 us
  blocking collectives  221 us (48%)
  waiting for transfers between devices  163 us (35%)
  other arithmetic  19.6 us (4%)
  starting transfers between devices  17.9 us (4%)
  matrix products  17 us (4%)
  between operations  15.6 us (3%)
  local copies, waits for them, and re-layouts  5.76 us (1%)
    psum x2, waiting for transfers between devices, shards(): correction = lax.psum(local_correction, 'var')  148 us
    all_to_all x2, blocking collectives, summed_on_arrival(): lax.all_to_all(blocks, axis, split_axis=0, concat_axis=0, tiled=True)  120 us
    all_to_all x4, blocking collectives, from_everyone(): lax.all_to_all(jnp.broadcast_to(array[None], (size, *array.shape)), axis,...  101 us
    all_to_all x2, starting transfers between devices, from_everyone(): lax.all_to_all(jnp.broadcast_to(array[None], (size, *array.shape)), axis,...  17.8 us
    all_to_all x2, waiting for transfers between devices, from_everyone(): lax.all_to_all(jnp.broadcast_to(array[None], (size, *array.shape)), axis,...  14.9 us
    dot_general x2, matrix products, shards(): lax.dot_general(centered, change_rows, (((1,), (1,)), ((), ())), preferre...  9.39 us
  transfers between devices with their start and end apart: 4, of which 4 were waited for; matrix products, arithmetic and copies ran while one was open for 2% of the time, Pallas kernels for 0%

commit v1 on v0

v1 whole, which is shorter than its diff:
```python
import functools

import jax
import jax.numpy as jnp
from jax import lax
from jax.experimental import pallas as pl
from jax.experimental.pallas import tpu as pltpu
from jax.sharding import PartitionSpec as P

K = 256
BS = 2048
ROUNDS = 2
SAMPLES = 34560
ROWS = 1080
PAD = 1152
NS = 32
NT = 16
NV = 8
W = 128
YR = 272
MESH = pl.DeviceIdType.MESH
F32 = jnp.float32
BF16 = jnp.bfloat16


def al(x, m):
    return pl.multiple_of(x, m)


def kernel(
    colors, x_hbm, res_hbm, coef, pen,
    coef_out, res_out,
    xs, tail, rf, rt, rsum, g, st_loc, st_in, st_own, stats, mhl,
    oldb, newb, newt,
    pair_tx, pair_rx, rs_tx, rs_rx, nrm, dmat, c_tx, c_rx, t_buf,
    x_sem, r_sem,
    st_ss, st_rs, sa_ss, sa_rs, old_ss, old_rs, new_ss, new_rs,
    pr_ss, pr_rs, rs_ss, rs_rs, nm_ss, nm_rs, ag_ss, ag_rs, fw_ss, fw_rs,
    cr_ss, cr_rs, ca_ss, ca_rs,
):
    s = lax.axis_index("samp")
    v = lax.axis_index("var")
    t = s // 2
    c = s % 2
    half = s // 16
    partner = s + 1 - 2 * c

    def rcopy(src, dst, ss, rs, samp, var):
        return pltpu.make_async_remote_copy(
            src_ref=src, dst_ref=dst, send_sem=ss, recv_sem=rs,
            device_id=(samp, var), device_id_type=MESH,
        )

    xcopies = []
    for q in range(4):
        xcopies.append(pltpu.make_async_copy(
            x_hbm.at[pl.ds(0, 1072), pl.ds(q * 1024, 1024)],
            xs.at[q // 2, pl.ds(0, 1072), pl.ds(q % 2 * 1024, 1024)], x_sem.at[q]))
        xcopies[-1].start()
    tcopy = pltpu.make_async_copy(x_hbm.at[pl.ds(1072, 8), :], tail, x_sem.at[4])
    tcopy.start()
    rcopy_in = pltpu.make_async_copy(res_hbm, rf.at[pl.ds(0, ROWS), :], r_sem)
    rcopy_in.start()

    barrier = pltpu.get_barrier_semaphore()

    @pl.loop(1, NS)
    def _(i):
        pl.semaphore_signal(barrier, inc=1, device_id=((s + i) % NS, v), device_id_type=MESH)

    @pl.loop(1, NV)
    def _(i):
        pl.semaphore_signal(barrier, inc=1, device_id=(s, (v + i) % NV), device_id_type=MESH)

    rf[pl.ds(ROWS, PAD - ROWS), :] = jnp.zeros((PAD - ROWS, K), F32)
    tcopy.wait()
    for b in range(2):
        xs[b, pl.ds(1088, PAD - 1088), :] = jnp.zeros((PAD - 1088, BS), BF16)
        xs[b, pl.ds(1072, 16), :] = jnp.concatenate(
            [tail[:, pl.ds(b * BS, BS)].astype(F32), jnp.zeros((8, BS), F32)], axis=0).astype(BF16)

    for q in range(4):
        xcopies[q].wait()

        @pl.loop(0, 4)
        def _(u):
            lanes = pl.ds(al(q % 2 * 1024 + u * 256, 256), 256)
            cnt = jnp.zeros((16, 256), F32)
            sqr = jnp.zeros((16, 256), F32)
            for h in range(2):
                b = xs[q // 2, pl.ds(h * 576, 16), lanes]
                a = b
                d = b * b
                for i in range(1, 36):
                    b = xs[q // 2, pl.ds(h * 576 + i * 16, 16), lanes]
                    a = a + b
                    d = d + b * b
                cnt = cnt + a.astype(F32)
                sqr = sqr + d.astype(F32)
            st_loc[q // 2, pl.ds(0, 1), lanes] = jnp.sum(cnt, axis=0, keepdims=True)
            st_loc[q // 2, pl.ds(1, 1), lanes] = jnp.sum(sqr, axis=0, keepdims=True)

    pl.semaphore_wait(barrier, NS - 1 + NV - 1)

    def st_send(p):
        return rcopy(st_loc.at[p // 16, :, pl.ds(al(p % 16 * W, W), W)], st_in.at[s], st_ss.at[p], st_rs.at[s], p, v)

    @pl.loop(1, NS)
    def _(i):
        st_send((s + i) % NS).start()

    st_in[s] = st_loc[half, :, pl.ds(al(s % 16 * W, W), W)]

    def old_send(b, j):
        return (coef.at[:, pl.ds(al(b * BS + j * W, W), W)],
                oldb.at[b, pl.ds(al((s % 16) * 8, 8), 8), :])

    for b in range(2):
        @pl.loop(0, NT)
        def _(i):
            j = (t + i) % NT
            dest = 2 * j + half
            src, dst = old_send(b, j)

            @pl.when(dest != s)
            def _():
                rcopy(src, dst, old_ss.at[b, j], old_rs.at[b, s % 16], dest, v).start()

            @pl.when(dest == s)
            def _():
                oldb[b, pl.ds(al((s % 16) * 8, 8), 8), :] = coef[:, pl.ds(al(b * BS + j * W, W), W)]

    def transposed():
        for i in range(PAD // W):
            rt[:, pl.ds(i * W, W)] = rf[pl.ds(i * W, W), :].T.astype(BF16)
        rsum[...] = jnp.broadcast_to(
            jnp.sum(rt[...].astype(F32), axis=1, keepdims=True), (K, W))

    def products(color):
        @pl.loop(0, 8)
        def _(u):
            lanes = pl.ds(al(u * 256, 256), 256)
            g[:, lanes] = jnp.dot(rt[...], xs[color, :, lanes], preferred_element_type=F32)

    oldb[2] = jnp.zeros((W, W), F32)
    for b in range(2):
        newt[2 + b] = coef[:, pl.ds(b * BS, BS)]
    rcopy_in.wait()
    transposed()
    products(colors[0, 0])

    @pl.loop(1, NS)
    def _(i):
        p = (s + i) % NS
        rcopy(st_loc.at[0, :, pl.ds(0, W)], st_in.at[p], st_ss.at[p], st_rs.at[p], p, v).wait_recv()

    total = jnp.sum(st_in[...], axis=0)
    mean_own = total[0:1] / SAMPLES
    st_own[pl.ds(0, 1), :] = mean_own
    st_own[pl.ds(1, 1), :] = total[1:2] - total[0:1] * mean_own

    def sa_send(p):
        return rcopy(st_own, stats.at[half, :, pl.ds(al(s % 16 * W, W), W)], sa_ss.at[p], sa_rs.at[s], p, v)

    @pl.loop(1, NS)
    def _(i):
        sa_send((s + i) % NS).start()

    stats[half, :, pl.ds(al(s % 16 * W, W), W)] = st_own[...]

    @pl.loop(1, NS)
    def _(i):
        p = (s + i) % NS
        rcopy(st_own, stats.at[p // 16, :, pl.ds(al(p % 16 * W, W), W)], sa_ss.at[p], sa_rs.at[p], p, v).wait_recv()

    for b in range(2):
        mean_all = stats[b, pl.ds(0, 1), :]
        high = mean_all.astype(BF16).astype(F32)
        mhl[b] = jnp.concatenate(
            [jnp.broadcast_to(high, (8, BS)), jnp.broadcast_to(mean_all - high, (8, BS))],
            axis=0).astype(BF16)

    own_rows = pl.ds(al(c * W, W), W)
    other_rows = pl.ds(al((1 - c) * W, W), W)
    own_lanes = pl.ds(al(t * W, W), W)

    def new_copy(r, i):
        return (newb.at[r, pl.ds(al(i * 8, 8), 8), :], newt.at[r, :, own_lanes])

    for r in range(ROUNDS):
        color = colors[r, 0]
        if r > 0:
            transposed()
            products(color)

        def pair_copy(u):
            lanes = pl.ds(al(u * 512, 512), 512)
            return rcopy(pair_tx.at[r, :, lanes], pair_rx.at[r, :, lanes],
                         pr_ss.at[r, u], pr_rs.at[r, u], partner, v)

        @pl.loop(0, 4)
        def _(u):
            lanes = pl.ds(al(u * 512, 512), 512)
            mean = stats[color, pl.ds(0, 1), lanes]
            rs_o = rsum[other_rows, :][:, 0:1]
            pair_tx[r, :, lanes] = (g[other_rows, lanes] - rs_o * mean).astype(BF16)
            pair_copy(u).start()

        def rs_copy(j, i_src):
            return rcopy(rs_tx.at[r, j], rs_rx.at[r, i_src], rs_ss.at[r, j], rs_rs.at[r, i_src], 2 * j + c, v)

        @pl.loop(0, 4)
        def _(u):
            lanes = pl.ds(al(u * 512, 512), 512)
            mean = stats[color, pl.ds(0, 1), lanes]
            rs_o = rsum[own_rows, :][:, 0:1]
            mine = g[own_rows, lanes] - rs_o * mean
            pair_copy(u).wait_recv()
            mine = mine + pair_rx[r, :, lanes].astype(F32)
            g[own_rows, lanes] = mine
            low = mine.astype(BF16)
            for w in range(4):
                rs_tx[r, u * 4 + w] = low[:, w * W:(w + 1) * W]
            for w in range(4):
                j = u * 4 + w

                @pl.when(j != t)
                def _():
                    rs_copy(j, t).start()

        newb[r] = g[own_rows, own_lanes]

        @pl.loop(1, NT)
        def _(i):
            j = (t + i) % NT
            rs_copy(j, j).wait_recv()
            newb[r] = newb[r] + rs_rx[r, j].astype(F32)

        if r == 0:
            for b in range(2):
                @pl.loop(0, 16)
                def _(i):
                    src_dev = 16 * c + i

                    @pl.when(src_dev != s)
                    def _():
                        rcopy(coef.at[:, pl.ds(0, W)], oldb.at[b, pl.ds(al(i * 8, 8), 8), :],
                              old_ss.at[b, i], old_rs.at[b, i], src_dev, v).wait_recv()
            old = oldb[color]
        else:
            gap = color - colors[0, 0]
            old = oldb[color + (1 - gap * gap) * (2 - color)]
        scale = stats[color, pl.ds(1, 1), own_lanes]
        shifted = old + newb[r] / scale
        part = jnp.sum(shifted * shifted, axis=0, keepdims=True)
        nrm[r, 0] = jnp.broadcast_to(part, (8, W))
        ncopy = rcopy(nrm.at[r, 0], nrm.at[r, 1], nm_ss.at[r], nm_rs.at[r], partner, v)
        ncopy.start()
        push = pen[color, :, own_lanes] * jnp.sqrt(K / scale)
        ncopy.wait_recv()
        norm = jnp.sqrt(part + nrm[r, 1][0:1] + 1e-06)
        new = jnp.maximum(0.0, 1.0 - push / norm) * shifted
        dmat[r, own_rows, own_lanes] = (new - old).astype(BF16)
        newb[r] = new
        if r == 0:
            oldb[2] = new

        def d_view(core, j):
            return dmat.at[r, pl.ds(al(core * W, W), W), pl.ds(al(j * W, W), W)]

        def ag_copy(j, i_src):
            return rcopy(d_view(c, i_src), d_view(c, i_src), ag_ss.at[r, j], ag_rs.at[r, i_src], 2 * j + c, v)

        def fw_copy(core, j):
            return rcopy(d_view(core, j), d_view(core, j), fw_ss.at[r, j], fw_rs.at[r, j], partner, v)

        @pl.loop(1, NT)
        def _(i):
            ag_copy((t + i) % NT, t).start()

        fw_copy(c, t).start()

        @pl.loop(0, 16)
        def _(i):
            dest = 16 * c + i
            src, dst = new_copy(r, i)

            @pl.when(dest != s)
            def _():
                rcopy(src, dst, new_ss.at[r, i], new_rs.at[r, t], dest, v).start()

            @pl.when(dest == s)
            def _():
                newt[r, :, own_lanes] = newb[r, pl.ds(al(i * 8, 8), 8), :]

        @pl.loop(1, NT)
        def _(i):
            j = (t + i) % NT
            ag_copy(j, j).wait_recv()
            fw_copy(c, j).start()

        @pl.loop(0, NT)
        def _(i):
            fw_copy(1 - c, (t + i) % NT).wait_recv()

        nt = (((1,), (1,)), ((), ()))
        md = lax.dot_general(mhl[color], dmat[r], nt, preferred_element_type=F32)
        md = md[0:1] + md[8:9]
        yv = v % 4
        xv = v // 4

        def cr_copy(p):
            return rcopy(c_tx.at[r, p], c_rx.at[r, v], cr_ss.at[r, p], cr_rs.at[r, v], p_samp, p)

        p_samp = s

        @pl.loop(0, 4)
        def _(i):
            y = (yv + 1 + i) % 4
            out = lax.dot_general(xs[color, pl.ds(al(y * YR, 16), YR), :], dmat[r], nt,
                                  preferred_element_type=F32) - md
            for w in range(2):
                c_tx[r, w * 4 + y] = out[:, w * W:(w + 1) * W].astype(BF16)
            for w in range(2):
                p = w * 4 + y

                @pl.when(p != v)
                def _():
                    cr_copy(p).start()

        def cr_recv(p):
            return rcopy(c_tx.at[r, p], c_rx.at[r, p], cr_ss.at[r, p], cr_rs.at[r, p], s, p)

        g[pl.ds(0, 256), pl.ds(0, W)] = c_tx[r, v, pl.ds(0, 256), :].astype(F32)
        g[pl.ds(0, 16), pl.ds(W, W)] = c_tx[r, v, pl.ds(256, 16), :].astype(F32)

        @pl.loop(1, NV)
        def _(i):
            p = (v + i) % NV
            cr_recv(p).wait_recv()
            g[pl.ds(0, 256), pl.ds(0, W)] += c_rx[r, p, pl.ds(0, 256), :].astype(F32)
            g[pl.ds(0, 16), pl.ds(W, W)] += c_rx[r, p, pl.ds(256, 16), :].astype(F32)

        t_buf[r, v, pl.ds(0, 256), :] = g[pl.ds(0, 256), pl.ds(0, W)].astype(BF16)
        t_buf[r, v, pl.ds(256, 16), :] = g[pl.ds(0, 16), pl.ds(W, W)].astype(BF16)

        def ca_copy(p, i_src):
            return rcopy(t_buf.at[r, i_src], t_buf.at[r, i_src], ca_ss.at[r, p], ca_rs.at[r, i_src], s, p)

        @pl.loop(1, NV)
        def _(i):
            ca_copy((v + i) % NV, v).start()

        def subtract(p):
            for w in range(2):
                @pl.when(p // 4 == w)
                def _():
                    rows = pl.ds(al((p % 4) * YR, 16), YR)
                    lanes = pl.ds(w * W, W)
                    rf[rows, lanes] = rf[rows, lanes] - t_buf[r, p].astype(F32)

        subtract(v)

        @pl.loop(1, NV)
        def _(i):
            p = (v + i) % NV
            ca_copy(p, p).wait_recv()
            subtract(p)

        rf[pl.ds(ROWS, 8), :] = jnp.zeros((8, K), F32)

    res_out[...] = rf[pl.ds(0, ROWS), :]

    for r in range(ROUNDS):
        @pl.loop(0, NT)
        def _(i):
            @pl.when(2 * i + half != s)
            def _():
                rcopy(newb.at[r, pl.ds(0, 8), :], newt.at[r, :, pl.ds(al(i * W, W), W)],
                      new_ss.at[r, i], new_rs.at[r, i], 2 * i + half, v).wait_recv()

    for b in range(2):
        lanes = pl.ds(b * BS, BS)
        d0 = colors[0, 0] - b
        d1 = colors[1, 0] - b
        coef_out[:, lanes] = newt[1 - d1 * d1 + d1 * d1 * d0 * d0 * (2 + b)]

    @pl.loop(1, NS)
    def _(i):
        p = (s + i) % NS
        st_send(p).wait_send()
        sa_send(p).wait_send()

    for b in range(2):
        @pl.loop(0, NT)
        def _(j):
            @pl.when(2 * j + half != s)
            def _():
                src, dst = old_send(b, j)
                rcopy(src, dst, old_ss.at[b, j], old_rs.at[b, s % 16], 2 * j + half, v).wait_send()

    for r in range(ROUNDS):
        @pl.loop(0, 4)
        def _(u):
            lanes = pl.ds(al(u * 512, 512), 512)
            rcopy(pair_tx.at[r, :, lanes], pair_rx.at[r, :, lanes],
                  pr_ss.at[r, u], pr_rs.at[r, u], partner, v).wait_send()

        rcopy(nrm.at[r, 0], nrm.at[r, 1], nm_ss.at[r], nm_rs.at[r], partner, v).wait_send()

        @pl.loop(0, 16)
        def _(i):
            @pl.when(16 * c + i != s)
            def _():
                src, dst = new_copy(r, i)
                rcopy(src, dst, new_ss.at[r, i], new_rs.at[r, t], 16 * c + i, v).wait_send()

        @pl.loop(0, NT)
        def _(j):
            view = dmat.at[r, own_rows, pl.ds(al(j * W, W), W)]
            rcopy(view, view, fw_ss.at[r, j], fw_rs.at[r, j], partner, v).wait_send()

            @pl.when(j != t)
            def _():
                rcopy(rs_tx.at[r, j], rs_rx.at[r, t], rs_ss.at[r, j], rs_rs.at[r, t], 2 * j + c, v).wait_send()
                mine = dmat.at[r, own_rows, own_lanes]
                rcopy(mine, mine, ag_ss.at[r, j], ag_rs.at[r, t], 2 * j + c, v).wait_send()

        @pl.loop(1, NV)
        def _(i):
            p = (v + i) % NV
            rcopy(c_tx.at[r, p], c_rx.at[r, v], cr_ss.at[r, p], cr_rs.at[r, v], s, p).wait_send()
            rcopy(t_buf.at[r, v], t_buf.at[r, v], ca_ss.at[r, p], ca_rs.at[r, v], s, p).wait_send()


def shards(genotypes, residual, coefficients, penalty, colors):
    dma = pltpu.SemaphoreType.DMA
    vm = pltpu.VMEM
    coef, res = pl.pallas_call(
        kernel,
        out_shape=(jax.ShapeDtypeStruct((8, 2 * BS), F32), jax.ShapeDtypeStruct((ROWS, K), F32)),
        in_specs=[
            pl.BlockSpec(memory_space=pltpu.SMEM),
            pl.BlockSpec(memory_space=pl.ANY),
            pl.BlockSpec(memory_space=pl.ANY),
            pl.BlockSpec(memory_space=pltpu.VMEM),
            pl.BlockSpec(memory_space=pltpu.VMEM),
        ],
        out_specs=[pl.BlockSpec(memory_space=pltpu.VMEM)] * 2,
        scratch_shapes=[
            vm((2, PAD, BS), BF16), vm((8, 2 * BS), BF16), vm((PAD, K), F32), vm((K, PAD), BF16),
            vm((K, W), F32), vm((K, BS), F32), vm((2, 2, BS), F32), vm((NS, 2, W), F32),
            vm((2, W), F32), vm((2, 2, BS), F32), vm((2, 16, BS), BF16),
            vm((3, W, W), F32), vm((2, W, W), F32), vm((4, 8, BS), F32),
            vm((2, W, BS), BF16), vm((2, W, BS), BF16),
            vm((2, NT, W, W), BF16), vm((2, NT, W, W), BF16), vm((2, 2, 8, W), F32),
            vm((2, K, BS), BF16),
            vm((2, NV, YR, W), BF16), vm((2, NV, YR, W), BF16), vm((2, NV, YR, W), BF16),
            dma((5,)), dma,
            dma((NS,)), dma((NS,)), dma((NS,)), dma((NS,)),
            dma((2, 16)), dma((2, 16)), dma((2, 16)), dma((2, 16)),
            dma((2, 4)), dma((2, 4)), dma((2, NT)), dma((2, NT)), dma((2,)), dma((2,)),
            dma((2, NT)), dma((2, NT)), dma((2, NT)), dma((2, NT)),
            dma((2, NV)), dma((2, NV)), dma((2, NV)), dma((2, NV)),
        ],
        compiler_params=pltpu.CompilerParams(
            collective_id=0, has_side_effects=True, vmem_limit_bytes=56 * 1024 * 1024),
    )(colors, genotypes, residual, coefficients, penalty.reshape(2, 1, BS))
    return (coef, res)


def solution(mesh):
    placed = (P("samp", "var"), P("samp", None), P("samp", "var"), P("var"), P(None, "var"))
    return jax.shard_map(
        shards,
        mesh=mesh,
        in_specs=placed,
        out_specs=(P("samp", "var"), P("samp", None)),
        check_vma=False,
    )
```

time: 464 us -> 153 us (0.33)
  blocking collectives: 221 us -> 0 us
  waiting for transfers between devices: 163 us -> 0 us
  Pallas kernels: 0 us -> 146 us
  other arithmetic: 19.6 us -> 0 us
  starting transfers between devices: 17.9 us -> 0 us
  matrix products: 17 us -> 0 us
  between operations: 15.6 us -> 0.64 us
    all_to_all x6 -> x0, blocking collectives: 221 us -> none  [the longest x2 120 us: summed_on_arrival(): lax.all_to_all(blocks, axis, split_axis=0, concat_axis=0, tiled=True)]
    psum x2 -> x0, waiting for transfers between devices: 148 us -> none  [shards(): correction = lax.psum(local_correction, 'var')]
    pallas_call x0 -> x1, Pallas kernels: none -> 146 us  [shards(): pl.pallas_call(kernel, out_shape=(jax.ShapeDtypeStruct((8, 2 * BS), F32),...]
    all_to_all x2 -> x0, starting transfers between devices: 17.8 us -> none  [from_everyone(): lax.all_to_all(jnp.broadcast_to(array[None], (size, *array.shape)), axis,...]
    dot_general x4 -> x0, matrix products: 17 us -> none  [the longest x2 9.39 us: shards(): lax.dot_general(centered, change_rows, (((1,), (1,)), ((), ())), preferre...]
    all_to_all x2 -> x0, waiting for transfers between devices: 14.9 us -> none  [from_everyone(): lax.all_to_all(jnp.broadcast_to(array[None], (size, *array.shape)), axis,...]
    reduce_sum x10 -> x0, other arithmetic: 11.3 us -> none  [the longest x1 5.3 us: column_moments(): squares = jnp.sum(wide * wide, axis=0)]
  transfers between devices with their start and end apart: 4 -> 0, of which waited for: 4 -> 0; matrix products, arithmetic and copies ran while one was open for 2% -> 0% of each run, Pallas kernels for 0% -> 0%
where the time goes in v1:
time: 153 us; the launch traced here: 152 us
  Pallas kernels  146 us (95%)
  local copies, waits for them, and re-layouts  5.17 us (3%)
    pallas_call x1, Pallas kernels, shards(): pl.pallas_call(kernel, out_shape=(jax.ShapeDtypeStruct((8, 2 * BS), F32),...  146 us
    unnamed x3, local copies, waits for them, and re-layouts  5.17 us

profile of v1, /device:TPU:1, one launch (start us, length us, event | category | flops | bytes accessed | tf_op | source)
XLA Modules:
  0.0 152.2 jit_solution(3719762612093016711)
XLA Ops:
  0.6 1.3 copy.7.colors
  1.9 146.4 %shard_map.68 = (f32[8,4096]{1,0:T(8,128)}, f32[1080,256]{1,0:T(8,128)}) custom-call(s32[2,1]{1,0:T(2,128)} %copy.7.colors, bf16[1080,4096]{1,0:T(8,128)(2,1)} %x_hbm.1, f32[1080,256]{1,0:T(8,128)} %res_hbm.1, f32[8,4096]{1,0:T(8,128)} %coef.1, f32[2,1,2048]{2,1,0:T(1,128)} %bitcast.1), custom_call_target="tpu_custom_call" | custom-call | tf_op jit(solution)/shard_map/pallas_call | solution.py:439
  148.4 1.6 %copy.10 = f32[8,4096]{1,0:T(8,128)} copy(f32[8,4096]{1,0:T(8,128)} %get-tuple-element.4) | data formatting | bytes 262144
  149.9 2.3 %copy.11 = f32[1080,256]{1,0:T(8,128)} copy(f32[1080,256]{1,0:T(8,128)} %get-tuple-element.5) | data formatting | bytes 2211840

commit v2 on v0

v2 whole, which is shorter than its diff:
```python
import jax
import jax.numpy as jnp
from jax import lax
from jax.experimental import pallas as pl
from jax.experimental.pallas import tpu as pltpu
from jax.sharding import PartitionSpec as P

K = 256
BS = 2048
ROUNDS = 2
SAMPLES = 34560
ROWS = 1080
PAD = 1152
NS = 32
NT = 16
NV = 8
W = 128
HW = 64
YR = 272
PR = 136
MESH = pl.DeviceIdType.MESH
F32 = jnp.float32
BF16 = jnp.bfloat16
NN_T = (((1,), (1,)), ((), ()))


def al(x, m):
    return pl.multiple_of(x, m)


def zigzag(a, middle):
    return middle + (1 - 2 * (a % 2)) * ((a + 1) // 2)


def split(x):
    high = x.astype(BF16).astype(F32)
    return high, x - high


def kernel(
    colors, x_hbm, res_hbm, coef, pen,
    coef_out, res_out,
    xs, tail, rf, rt, rsum, g, gacc, st_loc, st_in, rg_loc, rg_in, fix, mean_own, scale_own, means, mhl,
    cb, stage, oldr, pick, newb, newt,
    pair_tx, pair_rx, rs_tx, rs_rx, nrm, dmat, c_tx, c_rx, t_buf, tacc,
    x_sem, r_sem,
    st_ss, st_rs, rg_ss, rg_rs, mn_ss, mn_rs, old_ss, old_rs, new_ss, new_rs,
    pr_ss, pr_rs, rs_ss, rs_rs, nm_ss, nm_rs, ag_ss, ag_rs, fw_ss, fw_rs,
    cr_ss, cr_rs, ca_ss, ca_rs,
):
    s = lax.axis_index("samp")
    v = lax.axis_index("var")
    t = s // 2
    c = s % 2
    z = s // 4
    xh = t % 2
    yv = v % 4
    xv = v // 4
    partner = s + 1 - 2 * c
    holder = (s // 8) % 2
    place = pl.ds(al((s // 16) * HW + (s % 8) * 8, 8), 8)
    own_lanes = pl.ds(al(t * W, W), W)

    def chip(i):
        return ((z + zigzag(i // 2, 4)) % 8) * 2 + (xh + 1 - i % 2) % 2

    def group(i):
        return ((xv + 1 - i % 2) % 2) * 4 + (yv + zigzag(i // 2, 2)) % 4

    def rcopy(src, dst, ss, rs, samp, var):
        return pltpu.make_async_remote_copy(
            src_ref=src, dst_ref=dst, send_sem=ss, recv_sem=rs,
            device_id=(samp, var), device_id_type=MESH,
        )

    xcopies = []
    for q in range(4):
        xcopies.append(pltpu.make_async_copy(
            x_hbm.at[pl.ds(0, 1072), pl.ds(q * 1024, 1024)],
            xs.at[q // 2, pl.ds(0, 1072), pl.ds(q % 2 * 1024, 1024)], x_sem.at[q]))
    tcopy = pltpu.make_async_copy(x_hbm.at[pl.ds(1072, 8), :], tail, x_sem.at[4])
    rcopy_in = pltpu.make_async_copy(res_hbm, rf.at[pl.ds(0, ROWS), :], r_sem)
    rcopy_in.start()
    tcopy.start()
    for q in range(4):
        xcopies[q].start()

    barrier = pltpu.get_barrier_semaphore()

    @pl.loop(1, NS)
    def _(i):
        pl.semaphore_signal(barrier, inc=1, device_id=((s + i) % NS, v), device_id_type=MESH)

    @pl.loop(1, NV)
    def _(i):
        pl.semaphore_signal(barrier, inc=1, device_id=(s, (v + i) % NV), device_id_type=MESH)

    for b in range(2):
        cb[b] = coef[:, pl.ds(b * BS, BS)]
        newt[2 + b] = coef[:, pl.ds(b * BS, BS)]
    for r in range(ROUNDS):
        stage[r] = cb[colors[0, r]]

    def transposed(h):
        rows = pl.ds(h * W, W)
        for i in range(PAD // W):
            rt[rows, pl.ds(i * W, W)] = rf[pl.ds(i * W, W), pl.ds(h * W, W)].T.astype(BF16)
        rsum[rows, :] = jnp.broadcast_to(
            jnp.sum(rt[rows, :].astype(F32), axis=1, keepdims=True), (W, W))

    rf[pl.ds(ROWS, PAD - ROWS), :] = jnp.zeros((PAD - ROWS, K), F32)
    rcopy_in.wait()
    transposed(0)
    transposed(1)
    for h in range(2):
        rg_loc[pl.ds(h, 1), :] = jnp.sum(
            rf[:, pl.ds(h * W, W)].astype(BF16).astype(F32), axis=0, keepdims=True)
    tcopy.wait()
    for b in range(2):
        xs[b, pl.ds(1088, PAD - 1088), :] = jnp.zeros((PAD - 1088, BS), BF16)
        xs[b, pl.ds(1072, 16), :] = jnp.concatenate(
            [tail[:, pl.ds(b * BS, BS)].astype(F32), jnp.zeros((8, BS), F32)], axis=0).astype(BF16)

    for q in range(4):
        xcopies[q].wait()

        @pl.loop(0, 4)
        def _(u):
            lanes = pl.ds(al(q % 2 * 1024 + u * 256, 256), 256)
            cnt = jnp.zeros((16, 256), F32)
            sqr = jnp.zeros((16, 256), F32)
            for h in range(2):
                b = xs[q // 2, pl.ds(h * 576, 16), lanes]
                a = b
                d = b * b
                for i in range(1, 36):
                    b = xs[q // 2, pl.ds(h * 576 + i * 16, 16), lanes]
                    a = a + b
                    d = d + b * b
                cnt = cnt + a.astype(F32)
                sqr = sqr + d.astype(F32)
            st_loc[q // 2, pl.ds(0, 1), lanes] = jnp.sum(cnt, axis=0, keepdims=True)
            st_loc[q // 2, pl.ds(1, 1), lanes] = jnp.sum(sqr, axis=0, keepdims=True)

    pl.semaphore_wait(barrier, NS - 1 + NV - 1)

    def st_copy(p, i_src):
        return rcopy(st_loc.at[:, :, pl.ds(al(p // 2 * W, W), W)], st_in.at[:, i_src],
                     st_ss.at[p], st_rs.at[i_src], p, v)

    def rg_copy(p, i_src):
        return rcopy(rg_loc, rg_in.at[i_src], rg_ss.at[p], rg_rs.at[i_src], p, v)

    @pl.loop(1, NS)
    def _(i):
        p = (s + i) % NS
        st_copy(p, s).start()
        rg_copy(p, s).start()

    st_in[:, s] = st_loc[:, :, own_lanes]
    rg_in[s] = rg_loc[...]

    def old_copy(r, j):
        return rcopy(stage.at[r, :, pl.ds(al(j * W, W), W)], oldr.at[r, place, :],
                     old_ss.at[r, j], old_rs.at[r, (s // 16) * 8 + s % 8], 2 * j + holder, v)

    def old_sends(r):
        @pl.loop(0, NT)
        def _(j):
            @pl.when(2 * j + holder != s)
            def _():
                old_copy(r, j).start()

            @pl.when(2 * j + holder == s)
            def _():
                oldr[r, place, :] = stage[r, :, pl.ds(al(j * W, W), W)]

    def old_drain(r):
        @pl.loop(0, NT)
        def _(j):
            @pl.when(2 * j + holder != s)
            def _():
                old_copy(r, j).wait_send()

    def sharer(i):
        return (i // 8) * 16 + c * 8 + i % 8

    def old_wait(r):
        @pl.loop(0, 16)
        def _(i):
            @pl.when(sharer(i) != s)
            def _():
                rcopy(stage.at[r, :, pl.ds(0, W)], oldr.at[r, pl.ds(al(i * 8, 8), 8), :],
                      old_ss.at[r, 0], old_rs.at[r, i], sharer(i), v).wait_recv()

    def new_copy(r, i):
        return rcopy(newb.at[r, pl.ds(al(i * 8, 8), 8), :], newt.at[r, :, own_lanes],
                     new_ss.at[r, i], new_rs.at[r, t], sharer(i), v)

    old_sends(0)

    def own_rows(h):
        return pl.ds(al(c * HW, HW), HW)

    def products(r, h):
        @pl.loop(0, 8)
        def _(u):
            lanes = pl.ds(al(u * 256, 256), 256)
            g[h, :, lanes] = jnp.dot(
                rt[pl.ds(h * W, W), :], xs[colors[0, r], :, lanes], preferred_element_type=F32)

    def centre(r, lanes):
        if r == 0:
            return st_loc[colors[0, r], pl.ds(0, 1), lanes] * (1.0 / ROWS)
        return means[colors[0, r], :, lanes]

    def pair_copy(r, h, u):
        lanes = pl.ds(al(u * 1024, 1024), 1024)
        return rcopy(pair_tx.at[r, h, :, lanes], pair_rx.at[r, h, :, lanes],
                     pr_ss.at[r, h, u], pr_rs.at[r, h, u], partner, v)

    def pair_sends(r, h):
        rows = pl.ds(al((1 - c) * HW, HW), HW)
        for u in range(2):
            for w in range(2):
                lanes = pl.ds(u * 1024 + w * 512, 512)
                rs_o = rsum[pl.ds(al(h * W + (1 - c) * HW, HW), HW), :][:, 0:1]
                pair_tx[r, h, :, lanes] = (g[h, rows, lanes] - rs_o * centre(r, lanes)).astype(BF16)
            pair_copy(r, h, u).start()

    def rs_copy(r, h, j, i_src):
        return rcopy(rs_tx.at[r, h, j], rs_rx.at[r, h, i_src], rs_ss.at[r, h, j], rs_rs.at[r, h, i_src],
                     2 * j + c, v)

    def rs_sends(r, h):
        rows = own_rows(h)
        for u in range(2):
            pair_copy(r, h, u).wait_recv()
            for w in range(2):
                lanes = pl.ds(u * 1024 + w * 512, 512)
                rs_o = rsum[pl.ds(al(h * W + c * HW, HW), HW), :][:, 0:1]
                mine = g[h, rows, lanes] - rs_o * centre(r, lanes) + pair_rx[r, h, :, lanes].astype(F32)
                g[h, rows, lanes] = mine
                low = mine.astype(BF16)
                for e in range(4):
                    rs_tx[r, h, u * 8 + w * 4 + e] = low[:, e * W:(e + 1) * W]

        @pl.loop(0, NT - 1)
        def _(i):
            rs_copy(r, h, chip(i), t).start()

    products(0, 0)
    pair_sends(0, 0)
    products(0, 1)
    pair_sends(0, 1)
    rs_sends(0, 0)
    rs_sends(0, 1)

    @pl.loop(1, NS)
    def _(i):
        p = (s + i) % NS
        st_copy(p, p).wait_recv()
        rg_copy(p, p).wait_recv()

    for b in range(2):
        total = jnp.sum(st_in[b], axis=0)
        mean = total[0:1] / SAMPLES
        mean_own[b] = mean
        means[b, :, own_lanes] = mean
        scale_own[b] = total[1:2] - total[0:1] * mean

    def mn_copy(j, i_src):
        return rcopy(mean_own, means.at[:, :, pl.ds(al(i_src * W, W), W)], mn_ss.at[j], mn_rs.at[i_src],
                     2 * j + c, v)

    @pl.loop(0, NT - 1)
    def _(i):
        mn_copy(chip(i), t).start()

    b_high, b_low = split(st_in[colors[0, 0]][:, 0, :] * (1.0 / ROWS) - mean_own[colors[0, 0]])
    right = jnp.concatenate([b_high, b_low, b_high, b_low], axis=0).astype(BF16)
    for h in range(2):
        a_high, a_low = split(rg_in[:, h, :])
        left = jnp.concatenate([a_high, a_high, a_low, a_low], axis=0)
        fix[h] = jnp.dot(left.T.astype(BF16), right, preferred_element_type=F32)

    for r in range(ROUNDS):
        color = colors[0, r]

        for h in range(2):
            rows = pl.ds(h * HW, HW)
            if r == 0:
                gacc[rows, :] = g[h, own_rows(h), own_lanes] + fix[h, own_rows(h), :]
            else:
                gacc[rows, :] = g[h, own_rows(h), own_lanes]

            @pl.loop(0, NT - 1)
            def _(i):
                j = chip(i)
                rs_copy(r, h, j, j).wait_recv()
                gacc[rows, :] = gacc[rows, :] + rs_rx[r, h, j].astype(F32)

        old_wait(r)
        if r == 0:
            old = oldr[0]
        else:
            pick[0] = oldr[1]
            gap = color - colors[0, 0]
            old = pick[1 - gap * gap]
        scale = scale_own[color]
        shifted = old + gacc[...] / scale
        part = jnp.sum(shifted * shifted, axis=0, keepdims=True)
        nrm[r, 0] = jnp.broadcast_to(part, (8, W))
        ncopy = rcopy(nrm.at[r, 0], nrm.at[r, 1], nm_ss.at[r], nm_rs.at[r], partner, v)
        ncopy.start()
        push = pen[color, :, own_lanes] * jnp.sqrt(K / scale)
        ncopy.wait_recv()
        norm = jnp.sqrt(part + nrm[r, 1][0:1] + 1e-06)
        new = jnp.maximum(0.0, 1.0 - push / norm) * shifted
        change = (new - old).astype(BF16)
        for h in range(2):
            dmat[r, pl.ds(al(h * W + c * HW, HW), HW), own_lanes] = change[h * HW:(h + 1) * HW]
        newb[r] = new
        if r == 0:
            pick[1] = new

        def d_view(h, core, j):
            return dmat.at[r, pl.ds(al(h * W + core * HW, HW), HW), pl.ds(al(j * W, W), W)]

        def ag_copy(h, j, i_src):
            return rcopy(d_view(h, c, i_src), d_view(h, c, i_src), ag_ss.at[r, h, j], ag_rs.at[r, h, i_src],
                         2 * j + c, v)

        def fw_copy(h, core, j):
            return rcopy(d_view(h, core, j), d_view(h, core, j), fw_ss.at[r, h, j], fw_rs.at[r, h, j],
                         partner, v)

        for h in range(2):
            @pl.loop(0, NT - 1)
            def _(i):
                ag_copy(h, chip(i), t).start()

            fw_copy(h, c, t).start()

        if r == 0:
            @pl.loop(1, NS)
            def _(i):
                p = (s + i) % NS
                st_copy(p, s).wait_send()
                rg_copy(p, s).wait_send()

            old_drain(0)

            @pl.loop(0, NT - 1)
            def _(i):
                j = chip(i)
                mn_copy(j, j).wait_recv()
                mn_copy(j, t).wait_send()

            for b in range(2):
                high, low = split(means[b])
                mhl[b] = jnp.concatenate(
                    [jnp.broadcast_to(high, (8, BS)), jnp.broadcast_to(low, (8, BS))], axis=0).astype(BF16)
        ncopy.wait_send()
        for h in range(2):
            for u in range(2):
                pair_copy(r, h, u).wait_send()

            @pl.loop(0, NT - 1)
            def _(i):
                rs_copy(r, h, chip(i), t).wait_send()

        def cr_copy(h, p, i_src):
            return rcopy(c_tx.at[r, h, p], c_rx.at[r, h, i_src], cr_ss.at[r, h, p], cr_rs.at[r, h, i_src], s, p)

        for h in range(2):
            @pl.loop(0, NT - 1)
            def _(i):
                j = chip(i)
                ag_copy(h, j, j).wait_recv()
                fw_copy(h, c, j).start()

            @pl.loop(0, NT)
            def _(i):
                fw_copy(h, 1 - c, chip(i)).wait_recv()

            rows = pl.ds(h * W, W)
            md = lax.dot_general(mhl[color], dmat[r, rows, :], NN_T, preferred_element_type=F32)
            md = md[0:1] + md[8:9]

            @pl.loop(0, 4)
            def _(i):
                y = (yv + zigzag(i, 2)) % 4
                out = lax.dot_general(xs[color, pl.ds(al(y * YR, 16), YR), :], dmat[r, rows, :], NN_T,
                                      preferred_element_type=F32) - md
                for w in range(2):
                    c_tx[r, h, w * 4 + y] = out[w * PR:(w + 1) * PR].astype(BF16)
                for w in range(2):
                    p = w * 4 + y

                    @pl.when(p != v)
                    def _():
                        cr_copy(h, p, v).start()

        @pl.loop(0, 16)
        def _(i):
            @pl.when(sharer(i) != s)
            def _():
                new_copy(r, i).start()

            @pl.when(sharer(i) == s)
            def _():
                newt[r, :, own_lanes] = newb[r, pl.ds(al(i * 8, 8), 8), :]

        if r == 0:
            old_sends(1)

        def ca_copy(h, p, i_src):
            return rcopy(t_buf.at[r, h, i_src], t_buf.at[r, h, i_src], ca_ss.at[r, h, p], ca_rs.at[r, h, i_src],
                         s, p)

        for h in range(2):
            tacc[...] = c_tx[r, h, v].astype(F32)

            @pl.loop(0, NV - 1)
            def _(i):
                p = group(i)
                cr_copy(h, p, p).wait_recv()
                tacc[...] = tacc[...] + c_rx[r, h, p].astype(F32)

            t_buf[r, h, v] = tacc[...].astype(BF16)

            @pl.loop(0, NV - 1)
            def _(i):
                ca_copy(h, group(i), v).start()

        for h in range(2):
            @pl.loop(0, NT - 1)
            def _(i):
                ag_copy(h, chip(i), t).wait_send()

            @pl.loop(0, NT)
            def _(i):
                fw_copy(h, c, chip(i)).wait_send()

            @pl.loop(0, NV - 1)
            def _(i):
                cr_copy(h, group(i), v).wait_send()

        for h in range(2):
            lanes = pl.ds(h * W, W)

            def subtract(p):
                rows = pl.ds(al((p % 4) * YR + (p // 4) * PR, 8), PR)
                rf[rows, lanes] = rf[rows, lanes] - t_buf[r, h, p].astype(F32)

            subtract(v)

            @pl.loop(0, NV - 1)
            def _(i):
                p = group(i)
                ca_copy(h, p, p).wait_recv()
                subtract(p)

            if r == 0:
                rf[pl.ds(ROWS, 8), lanes] = jnp.zeros((8, W), F32)
                transposed(h)
                products(1, h)
                pair_sends(1, h)
                rs_sends(1, h)
            else:
                res_out[:, lanes] = rf[pl.ds(0, ROWS), lanes]

    for r in range(ROUNDS):
        @pl.loop(0, NT)
        def _(j):
            @pl.when(2 * j + holder != s)
            def _():
                rcopy(newb.at[r, pl.ds(0, 8), :], newt.at[r, :, pl.ds(al(j * W, W), W)],
                      new_ss.at[r, 0], new_rs.at[r, j], 2 * j + holder, v).wait_recv()

    for b in range(2):
        d0 = colors[0, 0] - b
        d1 = colors[0, 1] - b
        coef_out[:, pl.ds(b * BS, BS)] = newt[1 - d1 * d1 + d1 * d1 * d0 * d0 * (2 + b)]

    old_drain(1)
    for r in range(ROUNDS):
        @pl.loop(0, 16)
        def _(i):
            @pl.when(sharer(i) != s)
            def _():
                new_copy(r, i).wait_send()

        for h in range(2):
            @pl.loop(0, NV - 1)
            def _(i):
                p = group(i)
                rcopy(t_buf.at[r, h, v], t_buf.at[r, h, v], ca_ss.at[r, h, p], ca_rs.at[r, h, v],
                      s, p).wait_send()


def shards(genotypes, residual, coefficients, penalty, colors):
    dma = pltpu.SemaphoreType.DMA
    vm = pltpu.VMEM
    coef, res = pl.pallas_call(
        kernel,
        out_shape=(jax.ShapeDtypeStruct((8, 2 * BS), F32), jax.ShapeDtypeStruct((ROWS, K), F32)),
        in_specs=[
            pl.BlockSpec(memory_space=pltpu.SMEM),
            pl.BlockSpec(memory_space=pl.ANY),
            pl.BlockSpec(memory_space=pl.ANY),
            pl.BlockSpec(memory_space=pltpu.VMEM),
            pl.BlockSpec(memory_space=pltpu.VMEM),
        ],
        out_specs=[pl.BlockSpec(memory_space=pltpu.VMEM)] * 2,
        scratch_shapes=[
            vm((2, PAD, BS), BF16), vm((8, 2 * BS), BF16), vm((PAD, K), F32), vm((K, PAD), BF16),
            vm((K, W), F32), vm((2, W, BS), F32), vm((W, W), F32),
            vm((2, 2, BS), F32), vm((2, NS, 2, W), F32), vm((2, W), F32), vm((NS, 2, W), F32),
            vm((2, W, W), F32), vm((2, 1, W), F32), vm((2, 1, W), F32), vm((2, 1, BS), F32),
            vm((2, 16, BS), BF16),
            vm((2, 8, BS), F32), vm((2, 8, BS), F32), vm((2, W, W), F32), vm((2, W, W), F32),
            vm((2, W, W), F32), vm((4, 8, BS), F32),
            vm((2, 2, HW, BS), BF16), vm((2, 2, HW, BS), BF16),
            vm((2, 2, NT, HW, W), BF16), vm((2, 2, NT, HW, W), BF16), vm((2, 2, 8, W), F32),
            vm((2, K, BS), BF16),
            vm((2, 2, NV, PR, W), BF16), vm((2, 2, NV, PR, W), BF16), vm((2, 2, NV, PR, W), BF16),
            vm((PR, W), F32),
            dma((5,)), dma,
            dma((NS,)), dma((NS,)), dma((NS,)), dma((NS,)), dma((NT,)), dma((NT,)),
            dma((2, 16)), dma((2, 16)), dma((2, 16)), dma((2, 16)),
            dma((2, 2, 2)), dma((2, 2, 2)), dma((2, 2, NT)), dma((2, 2, NT)), dma((2,)), dma((2,)),
            dma((2, 2, NT)), dma((2, 2, NT)), dma((2, 2, NT)), dma((2, 2, NT)),
            dma((2, 2, NV)), dma((2, 2, NV)), dma((2, 2, NV)), dma((2, 2, NV)),
        ],
        compiler_params=pltpu.CompilerParams(
            collective_id=0, has_side_effects=True, vmem_limit_bytes=56 * 1024 * 1024),
    )(colors.T, genotypes, residual, coefficients, penalty.reshape(2, 1, BS))
    return (coef, res)


def solution(mesh):
    placed = (P("samp", "var"), P("samp", None), P("samp", "var"), P("var"), P(None, "var"))
    return jax.shard_map(
        shards,
        mesh=mesh,
        in_specs=placed,
        out_specs=(P("samp", "var"), P("samp", None)),
        check_vma=False,
    )
```

time: 464 us -> 124 us (0.27)
  blocking collectives: 221 us -> 0 us
  waiting for transfers between devices: 163 us -> 0 us
  Pallas kernels: 0 us -> 120 us
  other arithmetic: 19.6 us -> 0 us
  starting transfers between devices: 17.9 us -> 0 us
  matrix products: 17 us -> 0 us
  between operations: 15.6 us -> 0.64 us
    all_to_all x6 -> x0, blocking collectives: 221 us -> none  [the longest x2 120 us: summed_on_arrival(): lax.all_to_all(blocks, axis, split_axis=0, concat_axis=0, tiled=True)]
    psum x2 -> x0, waiting for transfers between devices: 148 us -> none  [shards(): correction = lax.psum(local_correction, 'var')]
    pallas_call x0 -> x1, Pallas kernels: none -> 120 us  [shards(): pl.pallas_call(kernel, out_shape=(jax.ShapeDtypeStruct((8, 2 * BS), F32),...]
    all_to_all x2 -> x0, starting transfers between devices: 17.8 us -> none  [from_everyone(): lax.all_to_all(jnp.broadcast_to(array[None], (size, *array.shape)), axis,...]
    dot_general x4 -> x0, matrix products: 17 us -> none  [the longest x2 9.39 us: shards(): lax.dot_general(centered, change_rows, (((1,), (1,)), ((), ())), preferre...]
    all_to_all x2 -> x0, waiting for transfers between devices: 14.9 us -> none  [from_everyone(): lax.all_to_all(jnp.broadcast_to(array[None], (size, *array.shape)), axis,...]
    reduce_sum x10 -> x0, other arithmetic: 11.3 us -> none  [the longest x1 5.3 us: column_moments(): squares = jnp.sum(wide * wide, axis=0)]
  transfers between devices with their start and end apart: 4 -> 0, of which waited for: 4 -> 0; matrix products, arithmetic and copies ran while one was open for 2% -> 0% of each run, Pallas kernels for 0% -> 0%
where the time goes in v2:
time: 124 us
  Pallas kernels  120 us (97%)
  local copies, waits for them, and re-layouts  3.87 us (3%)
    pallas_call x1, Pallas kernels, shards(): pl.pallas_call(kernel, out_shape=(jax.ShapeDtypeStruct((8, 2 * BS), F32),...  120 us
    unnamed x2, local copies, waits for them, and re-layouts  3.87 us

profile of v2, /device:TPU:1, one launch (start us, length us, event | category | flops | bytes accessed | tf_op | source)
XLA Modules:
  0.0 124.2 jit_solution(2047747207948270688)
XLA Ops:
  0.6 119.7 %shard_map.68 = (f32[8,4096]{1,0:T(8,128)}, f32[1080,256]{1,0:T(8,128)}) custom-call(s32[1,2]{1,0:T(1,128)} %bitcast.3, bf16[1080,4096]{1,0:T(8,128)(2,1)} %x_hbm.1, f32[1080,256]{1,0:T(8,128)} %res_hbm.1, f32[8,4096]{1,0:T(8,128)} %coef.1, f32[2,1,2048]{2,1,0:T(1,128)} %bitcast.2), custom_call_target="tpu_custom_call" | custom-call | tf_op jit(solution)/shard_map/pallas_call | solution.py:506
  120.3 1.6 %copy.9 = f32[8,4096]{1,0:T(8,128)} copy(f32[8,4096]{1,0:T(8,128)} %get-tuple-element.4) | data formatting | bytes 262144
  121.9 2.3 %copy.10 = f32[1080,256]{1,0:T(8,128)} copy(f32[1080,256]{1,0:T(8,128)} %get-tuple-element.5) | data formatting | bytes 2211840

commit v3 on v2

v3 whole, which is shorter than its diff:
```python
import jax
import jax.numpy as jnp
from jax import lax
from jax.experimental import pallas as pl
from jax.experimental.pallas import tpu as pltpu
from jax.sharding import PartitionSpec as P

K = 256
BS = 2048
ROUNDS = 2
SAMPLES = 34560
ROWS = 1080
PAD = 1152
NS = 32
NT = 16
NV = 8
W = 128
HW = 64
YR = 272
PR = 136
MESH = pl.DeviceIdType.MESH
F32 = jnp.float32
BF16 = jnp.bfloat16
NN_T = (((1,), (1,)), ((), ()))


def al(x, m):
    return pl.multiple_of(x, m)


def zigzag(a, middle):
    return middle + (1 - 2 * (a % 2)) * ((a + 1) // 2)


def split(x):
    high = x.astype(BF16).astype(F32)
    return high, x - high


def kernel(
    colors, x_hbm, res_hbm, coef, pen,
    coef_out, res_out,
    xs, tail, rf, rt, rsum, g, gacc, st_loc, st_in, rg_loc, rg_in, fix, mean_own, scale_own, means, mhl,
    cb, stage, oldr, pick, newb, newt,
    pair_tx, pair_rx, rs_tx, rs_rx, nrm, dmat, c_tx, c_rx, t_buf,
    x_sem, t_sem, r_sem,
    st_ss, st_rs, rg_ss, rg_rs, mn_ss, mn_rs, old_ss, old_rs, new_ss, new_rs,
    pr_ss, pr_rs, rs_ss, rs_rs, nm_ss, nm_rs, ag_ss, ag_rs, fw_ss, fw_rs,
    cr_ss, cr_rs, ca_ss, ca_rs,
):
    s = lax.axis_index("samp")
    v = lax.axis_index("var")
    t = s // 2
    c = s % 2
    z = s // 4
    xh = t % 2
    yv = v % 4
    xv = v // 4
    partner = s + 1 - 2 * c
    holder = (s // 8) % 2
    place = pl.ds(al((s // 16) * HW + (s % 8) * 8, 8), 8)
    own_lanes = pl.ds(al(t * W, W), W)

    def chip(i):
        return ((z + zigzag(i // 2, 4)) % 8) * 2 + (xh + 1 - i % 2) % 2

    def group(i):
        return ((xv + 1 - i % 2) % 2) * 4 + (yv + zigzag(i // 2, 2)) % 4

    def rcopy(src, dst, ss, rs, samp, var):
        return pltpu.make_async_remote_copy(
            src_ref=src, dst_ref=dst, send_sem=ss, recv_sem=rs,
            device_id=(samp, var), device_id_type=MESH,
        )

    def arrived(ref, sem):
        rcopy(ref, ref, sem, sem, partner, v).wait_recv()

    def departed(ref, sem):
        rcopy(ref, ref, sem, sem, partner, v).wait_send()

    def chunk(a):
        return pl.ds(al(((z + zigzag(a, 4)) % 8) * 256, 256), 256)

    def x_copy(b, a):
        return pltpu.make_async_copy(
            x_hbm.at[pl.ds(0, 1072), pl.ds(al(b * BS + ((z + zigzag(a, 4)) % 8) * 256, 256), 256)],
            xs.at[b, pl.ds(0, 1072), chunk(a)], x_sem.at[b, a])

    tcopy = pltpu.make_async_copy(x_hbm.at[pl.ds(1072, 8), :], tail, t_sem)
    rcopy_in = pltpu.make_async_copy(res_hbm, rf.at[pl.ds(0, ROWS), :], r_sem)
    rcopy_in.start()
    tcopy.start()

    @pl.loop(0, 8)
    def _(a):
        for b in range(2):
            x_copy(b, a).start()

    barrier = pltpu.get_barrier_semaphore()

    @pl.loop(1, NS)
    def _(i):
        pl.semaphore_signal(barrier, inc=1, device_id=((s + i) % NS, v), device_id_type=MESH)

    @pl.loop(1, NV)
    def _(i):
        pl.semaphore_signal(barrier, inc=1, device_id=(s, (v + i) % NV), device_id_type=MESH)

    for b in range(2):
        cb[b] = coef[:, pl.ds(b * BS, BS)]
        newt[2 + b] = coef[:, pl.ds(b * BS, BS)]
    for r in range(ROUNDS):
        stage[r] = cb[colors[0, r]]

    def transposed(h):
        for i in range(PAD // W):
            rt[h, pl.ds(0, W), pl.ds(i * W, W)] = rf[pl.ds(i * W, W), pl.ds(h * W, W)].T.astype(BF16)
        rsum[pl.ds(h * W, W), :] = jnp.broadcast_to(
            jnp.sum(rt[h, pl.ds(0, W), :].astype(F32), axis=1, keepdims=True), (W, W))

    rf[pl.ds(ROWS, PAD - ROWS), :] = jnp.zeros((PAD - ROWS, K), F32)
    for h in range(2):
        rt[h, pl.ds(W, 16), :] = jnp.ones((16, PAD), BF16)
    for r in range(ROUNDS):
        for h in range(2):
            rs_rx[r, h, t] = jnp.zeros((HW, W), BF16)
            c_rx[r, h, v] = jnp.zeros((PR, W), BF16)
    rcopy_in.wait()
    transposed(0)
    transposed(1)
    for h in range(2):
        rg_loc[pl.ds(h, 1), :] = jnp.sum(
            rf[:, pl.ds(h * W, W)].astype(BF16).astype(F32), axis=0, keepdims=True)
    tcopy.wait()
    for b in range(2):
        xs[b, pl.ds(1088, PAD - 1088), :] = jnp.zeros((PAD - 1088, BS), BF16)
        xs[b, pl.ds(1072, 16), :] = jnp.concatenate(
            [tail[:, pl.ds(b * BS, BS)].astype(F32), jnp.zeros((8, BS), F32)], axis=0).astype(BF16)

    def st_copy(p):
        return rcopy(st_loc.at[:, :, pl.ds(al(p // 2 * W, W), W)], st_in.at[:, s], st_ss, st_rs, p, v)

    def rg_copy(p):
        return rcopy(rg_loc, rg_in.at[s], rg_ss, rg_rs, p, v)

    def old_copy(r, j):
        return rcopy(stage.at[r, :, pl.ds(al(j * W, W), W)], oldr.at[r, place, :],
                     old_ss.at[r], old_rs.at[r], 2 * j + holder, v)

    def old_sends(r):
        @pl.loop(0, NT)
        def _(j):
            @pl.when(2 * j + holder != s)
            def _():
                old_copy(r, j).start()

            @pl.when(2 * j + holder == s)
            def _():
                oldr[r, place, :] = stage[r, :, pl.ds(al(j * W, W), W)]

    def each(wait, some, every):
        @pl.when(holder == c)
        def _():
            wait(some)

        @pl.when(holder != c)
        def _():
            wait(every)

    def old_drain(r):
        each(lambda ref: departed(ref, old_ss.at[r]), oldr.at[r, pl.ds(0, W - 8), :], oldr.at[r])

    def sharer(i):
        return (i // 8) * 16 + c * 8 + i % 8

    def old_wait(r):
        each(lambda ref: arrived(ref, old_rs.at[r]), oldr.at[r, pl.ds(0, W - 8), :], oldr.at[r])

    def new_copy(r, i):
        return rcopy(newb.at[r, pl.ds(al(i * 8, 8), 8), :], newt.at[r, :, own_lanes],
                     new_ss.at[r], new_rs.at[r], sharer(i), v)

    def new_wait(r):
        each(lambda ref: arrived(ref, new_rs.at[r]), newt.at[r, :, pl.ds(0, BS - W)], newt.at[r])

    def new_drain(r):
        each(lambda ref: departed(ref, new_ss.at[r]), newb.at[r, pl.ds(0, W - 8), :], newb.at[r])

    def ca_copy(r, h, p):
        return rcopy(t_buf.at[r, h, v], t_buf.at[r, h, v], ca_ss.at[r, h], ca_rs.at[r, h], s, p)

    def ca_drain(r, h):
        departed(t_buf.at[r, h, pl.ds(0, NV - 1)], ca_ss.at[r, h])

    def own_rows(h):
        return pl.ds(al(c * HW, HW), HW)

    def pair_copy(r, h, a):
        return rcopy(pair_tx.at[r, h, :, chunk(a)], pair_rx.at[r, h, :, chunk(a)],
                     pr_ss.at[r, h], pr_rs.at[r, h, a], partner, v)

    def moments(a):
        lanes = chunk(a)

        @pl.loop(0, 2)
        def _(b):
            cnt = jnp.zeros((16, 256), F32)
            sqr = jnp.zeros((16, 256), F32)
            for e in range(2):
                x = xs[b, pl.ds(e * 576, 16), lanes]
                one = x
                two = x * x
                for i in range(1, 36):
                    x = xs[b, pl.ds(e * 576 + i * 16, 16), lanes]
                    one = one + x
                    two = two + x * x
                cnt = cnt + one.astype(F32)
                sqr = sqr + two.astype(F32)
            st_loc[b, pl.ds(0, 1), lanes] = jnp.sum(cnt, axis=0, keepdims=True)
            st_loc[b, pl.ds(1, 1), lanes] = jnp.sum(sqr, axis=0, keepdims=True)

    def product(r, h, a, send=True):
        lanes = chunk(a)
        if r == 0:
            out = jnp.dot(rt[h], xs[colors[0, r], :, lanes], preferred_element_type=F32)
            mean = out[W:W + 1] * (1.0 / ROWS)
            out = out[:W]
        else:
            out = jnp.dot(rt[h, pl.ds(0, W), :], xs[colors[0, r], :, lanes], preferred_element_type=F32)
            mean = means[colors[0, r], :, lanes]
        g[h, :, lanes] = out - rsum[pl.ds(h * W, W), :][:, 0:1] * mean
        pair_tx[r, h, :, lanes] = g[h, pl.ds(al((1 - c) * HW, HW), HW), lanes].astype(BF16)
        if send:
            pair_copy(r, h, a).start()

    def rs_copy(r, h, j):
        return rcopy(rs_tx.at[r, h, j], rs_rx.at[r, h, t], rs_ss.at[r, h], rs_rs.at[r, h], 2 * j + c, v)

    def send_on(r, h, a):
        lanes = chunk(a)
        pair_copy(r, h, a).wait_recv()
        mine = g[h, own_rows(h), lanes] + pair_rx[r, h, :, lanes].astype(F32)
        g[h, own_rows(h), lanes] = mine
        low = mine.astype(BF16)
        for e in range(2):
            j = ((z + zigzag(a, 4)) % 8) * 2 + e
            rs_tx[r, h, j] = low[:, e * W:(e + 1) * W]

            @pl.when(j != t)
            def _():
                rs_copy(r, h, j).start()

    def gradient(r, h):
        @pl.loop(0, 4)
        def _(a):
            product(r, h, a, send=r + h > 0)

        if r + h == 0:
            pl.semaphore_wait(barrier, NS - 1 + NV - 1)

            @pl.loop(0, 4)
            def _(a):
                pair_copy(0, 0, a).start()

            @pl.loop(1, NS)
            def _(i):
                rg_copy((s + i) % NS).start()

            rg_in[s] = rg_loc[...]
            old_sends(0)

        @pl.loop(4, 8)
        def _(a):
            product(r, h, a)
            send_on(r, h, a - 4)

        @pl.loop(4, 8)
        def _(a):
            send_on(r, h, a)

    @pl.loop(0, 8)
    def _(a):
        for b in range(2):
            x_copy(b, a).wait()
        moments(a)

    gradient(0, 0)

    @pl.loop(1, NS)
    def _(i):
        st_copy((s + i) % NS).start()

    st_in[:, s] = st_loc[:, :, own_lanes]
    gradient(0, 1)

    def mn_copy(j):
        return rcopy(mean_own, means.at[:, :, own_lanes], mn_ss, mn_rs, 2 * j + c, v)

    st_all = st_in.at[:, pl.ds(0, NS - 1)]
    rg_all = rg_in.at[pl.ds(0, NS - 1)]
    mn_all = means.at[:, :, pl.ds(0, (NT - 1) * W)]

    def statistics():
        arrived(st_all, st_rs)
        arrived(rg_all, rg_rs)

        for b in range(2):
            total = jnp.sum(st_in[b], axis=0)
            mean = total[0:1] / SAMPLES
            mean_own[b] = mean
            means[b, :, own_lanes] = mean
            scale_own[b] = total[1:2] - total[0:1] * mean

        @pl.loop(0, NT - 1)
        def _(i):
            mn_copy(chip(i)).start()

        b_high, b_low = split(st_in[colors[0, 0]][:, 0, :] * (1.0 / ROWS) - mean_own[colors[0, 0]])
        right = jnp.concatenate([b_high, b_low, b_high, b_low], axis=0).astype(BF16)
        for h in range(2):
            a_high, a_low = split(rg_in[:, h, :])
            left = jnp.concatenate([a_high, a_high, a_low, a_low], axis=0)
            fix[h] = jnp.dot(left.T.astype(BF16), right, preferred_element_type=F32)
            gacc[pl.ds(h * HW, HW), :] = gacc[pl.ds(h * HW, HW), :] + fix[h, own_rows(h), :]

    def d_view(r, h, core, j):
        return dmat.at[r, pl.ds(al(h * W + core * HW, HW), HW), pl.ds(al(j * W, W), W)]

    def ag_copy(r, h, j, i_src):
        return rcopy(d_view(r, h, c, i_src), d_view(r, h, c, i_src), ag_ss.at[r, h], ag_rs.at[r, h, i_src],
                     2 * j + c, v)

    def fw_copy(r, h, j):
        return rcopy(d_view(r, h, c, j), d_view(r, h, c, j), fw_ss.at[r, h], fw_rs.at[r, h], partner, v)

    def cr_copy(r, h, p):
        return rcopy(c_tx.at[r, h, p], c_rx.at[r, h, v], cr_ss.at[r, h], cr_rs.at[r, h], s, p)

    def ag_drain(r):
        for h in range(2):
            departed(dmat.at[r, pl.ds(0, HW), pl.ds(0, (NT - 1) * W)], ag_ss.at[r, h])
            departed(dmat.at[r, pl.ds(0, HW), :], fw_ss.at[r, h])

    def cr_drain(r):
        for h in range(2):
            departed(c_tx.at[r, h, pl.ds(0, NV - 1)], cr_ss.at[r, h])

    for r in range(ROUNDS):
        color = colors[0, r]

        if r == 1:
            ag_drain(0)
            cr_drain(0)

        for h in range(2):
            rows = pl.ds(h * HW, HW)
            arrived(rs_rx.at[r, h, pl.ds(0, NT - 1)], rs_rs.at[r, h])
            total = g[h, own_rows(h), own_lanes]
            for j in range(NT):
                total = total + rs_rx[r, h, j].astype(F32)
            gacc[rows, :] = total

        old_wait(r)
        if r == 0:
            statistics()
            old = oldr[0]
        else:
            pick[0] = oldr[1]
            gap = color - colors[0, 0]
            old = pick[1 - gap * gap]
        scale = scale_own[color]
        shifted = old + gacc[...] / scale
        part = jnp.sum(shifted * shifted, axis=0, keepdims=True)
        nrm[r, 0] = jnp.broadcast_to(part, (8, W))
        ncopy = rcopy(nrm.at[r, 0], nrm.at[r, 1], nm_ss.at[r], nm_rs.at[r], partner, v)
        ncopy.start()
        push = pen[color, :, own_lanes] * jnp.sqrt(K / scale)
        ncopy.wait_recv()
        norm = jnp.sqrt(part + nrm[r, 1][0:1] + 1e-06)
        new = jnp.maximum(0.0, 1.0 - push / norm) * shifted
        change = (new - old).astype(BF16)
        for h in range(2):
            dmat[r, pl.ds(al(h * W + c * HW, HW), HW), own_lanes] = change[h * HW:(h + 1) * HW]
        newb[r] = new
        if r == 0:
            pick[1] = new

        for h in range(2):
            @pl.loop(0, NT - 1)
            def _(i):
                ag_copy(r, h, chip(i), t).start()

            fw_copy(r, h, t).start()

        if r == 0:
            departed(st_all, st_ss)
            departed(rg_all, rg_ss)
            departed(mn_all, mn_ss)
            old_drain(0)
            arrived(mn_all, mn_rs)
            for b in range(2):
                high, low = split(means[b])
                mhl[b] = jnp.concatenate(
                    [jnp.broadcast_to(high, (8, BS)), jnp.broadcast_to(low, (8, BS))], axis=0).astype(BF16)
        else:
            old_drain(1)
            new_drain(0)
            ca_drain(0, 0)
            ca_drain(0, 1)
        ncopy.wait_send()
        for h in range(2):
            departed(pair_tx.at[r, h], pr_ss.at[r, h])
            departed(rs_tx.at[r, h, pl.ds(0, NT - 1)], rs_ss.at[r, h])

        for h in range(2):
            @pl.loop(0, NT - 1)
            def _(i):
                j = chip(i)
                ag_copy(r, h, j, j).wait_recv()
                fw_copy(r, h, j).start()

            arrived(dmat.at[r, pl.ds(0, HW), :], fw_rs.at[r, h])

            rows = pl.ds(h * W, W)
            md = lax.dot_general(mhl[color], dmat[r, rows, :], NN_T, preferred_element_type=F32)
            md = md[0:1] + md[8:9]

            @pl.loop(0, 4)
            def _(i):
                y = (yv + zigzag(i, 2)) % 4
                out = lax.dot_general(xs[color, pl.ds(al(y * YR, 16), YR), :], dmat[r, rows, :], NN_T,
                                      preferred_element_type=F32) - md
                for w in range(2):
                    c_tx[r, h, w * 4 + y] = out[w * PR:(w + 1) * PR].astype(BF16)
                for w in range(2):
                    p = w * 4 + y

                    @pl.when(p != v)
                    def _():
                        cr_copy(r, h, p).start()

        def add_up(h):
            arrived(c_rx.at[r, h, pl.ds(0, NV - 1)], cr_rs.at[r, h])
            total = c_tx[r, h, v].astype(F32)
            for p in range(NV):
                total = total + c_rx[r, h, p].astype(F32)
            t_buf[r, h, v] = total.astype(BF16)

            @pl.loop(0, NV - 1)
            def _(i):
                ca_copy(r, h, group(i)).start()

        add_up(0)

        @pl.loop(0, 16)
        def _(i):
            @pl.when(sharer(i) != s)
            def _():
                new_copy(r, i).start()

            @pl.when(sharer(i) == s)
            def _():
                newt[r, :, own_lanes] = newb[r, pl.ds(al(i * 8, 8), 8), :]

        if r == 0:
            old_sends(1)
        else:
            ag_drain(1)

        add_up(1)

        if r == 1:
            cr_drain(r)

        if r == 1:
            new_wait(0)
            new_wait(1)

            for b in range(2):
                d0 = colors[0, 0] - b
                d1 = colors[0, 1] - b
                coef_out[:, pl.ds(b * BS, BS)] = newt[1 - d1 * d1 + d1 * d1 * d0 * d0 * (2 + b)]
            new_drain(r)

        for h in range(2):
            lanes = pl.ds(h * W, W)

            arrived(t_buf.at[r, h, pl.ds(0, NV - 1)], ca_rs.at[r, h])
            for p in range(NV):
                rows = pl.ds((p % 4) * YR + (p // 4) * PR, PR)
                rf[rows, lanes] = rf[rows, lanes] - t_buf[r, h, p].astype(F32)

            if r == 0:
                rf[pl.ds(ROWS, 8), lanes] = jnp.zeros((8, W), F32)
                transposed(h)
                gradient(1, h)
            else:
                res_out[:, lanes] = rf[pl.ds(0, ROWS), lanes]

    ca_drain(1, 0)
    ca_drain(1, 1)


def shards(genotypes, residual, coefficients, penalty, colors):
    dma = pltpu.SemaphoreType.DMA
    vm = pltpu.VMEM
    coef, res = pl.pallas_call(
        kernel,
        out_shape=(jax.ShapeDtypeStruct((8, 2 * BS), F32), jax.ShapeDtypeStruct((ROWS, K), F32)),
        in_specs=[
            pl.BlockSpec(memory_space=pltpu.SMEM),
            pl.BlockSpec(memory_space=pl.ANY),
            pl.BlockSpec(memory_space=pl.ANY),
            pl.BlockSpec(memory_space=pltpu.VMEM),
            pl.BlockSpec(memory_space=pltpu.VMEM),
        ],
        out_specs=[pl.BlockSpec(memory_space=pltpu.VMEM)] * 2,
        scratch_shapes=[
            vm((2, PAD, BS), BF16), vm((8, 2 * BS), BF16), vm((PAD, K), F32), vm((2, W + 16, PAD), BF16),
            vm((K, W), F32), vm((2, W, BS), F32), vm((W, W), F32),
            vm((2, 2, BS), F32), vm((2, NS, 2, W), F32), vm((2, W), F32), vm((NS, 2, W), F32),
            vm((2, W, W), F32), vm((2, 1, W), F32), vm((2, 1, W), F32), vm((2, 1, BS), F32),
            vm((2, 16, BS), BF16),
            vm((2, 8, BS), F32), vm((2, 8, BS), F32), vm((2, W, W), F32), vm((2, W, W), F32),
            vm((2, W, W), F32), vm((4, 8, BS), F32),
            vm((2, 2, HW, BS), BF16), vm((2, 2, HW, BS), BF16),
            vm((2, 2, NT, HW, W), BF16), vm((2, 2, NT, HW, W), BF16), vm((2, 2, 8, W), F32),
            vm((2, K, BS), BF16),
            vm((2, 2, NV, PR, W), BF16), vm((2, 2, NV, PR, W), BF16), vm((2, 2, NV, PR, W), BF16),
            dma((2, 8)), dma, dma,
            dma, dma, dma, dma, dma, dma, dma((2,)), dma((2,)), dma((2,)), dma((2,)),
            dma((2, 2)), dma((2, 2, 8)), dma((2, 2)), dma((2, 2)), dma((2,)), dma((2,)),
            dma((2, 2)), dma((2, 2, NT)), dma((2, 2)), dma((2, 2)),
            dma((2, 2)), dma((2, 2)), dma((2, 2)), dma((2, 2)),
        ],
        compiler_params=pltpu.CompilerParams(
            collective_id=0, has_side_effects=True, vmem_limit_bytes=56 * 1024 * 1024),
    )(colors.T, genotypes, residual, coefficients, penalty.reshape(2, 1, BS))
    return (coef, res)


def solution(mesh):
    placed = (P("samp", "var"), P("samp", None), P("samp", "var"), P("var"), P(None, "var"))
    return jax.shard_map(
        shards,
        mesh=mesh,
        in_specs=placed,
        out_specs=(P("samp", "var"), P("samp", None)),
        check_vma=False,
    )
```

time: 124 us -> 114 us (0.919)
  Pallas kernels: 120 us -> 109 us
    pallas_call x1, Pallas kernels: 120 us -> 109 us  [shards(): pl.pallas_call(kernel, out_shape=(jax.ShapeDtypeStruct((8, 2 * BS), F32),...]
where the time goes in v3:
time: 114 us; the launch traced here: 113 us
  Pallas kernels  109 us (96%)
  local copies, waits for them, and re-layouts  3.87 us (3%)
    pallas_call x1, Pallas kernels, shards(): pl.pallas_call(kernel, out_shape=(jax.ShapeDtypeStruct((8, 2 * BS), F32),...  109 us
    unnamed x2, local copies, waits for them, and re-layouts  3.87 us

profile of v3, /device:TPU:1, one launch (start us, length us, event | category | flops | bytes accessed | tf_op | source)
XLA Modules:
  0.0 113.5 jit_solution(10881561463024915173)
XLA Ops:
  0.6 109.0 %shard_map.68 = (f32[8,4096]{1,0:T(8,128)}, f32[1080,256]{1,0:T(8,128)}) custom-call(s32[1,2]{1,0:T(1,128)} %bitcast.3, bf16[1080,4096]{1,0:T(8,128)(2,1)} %x_hbm.1, f32[1080,256]{1,0:T(8,128)} %res_hbm.1, f32[8,4096]{1,0:T(8,128)} %coef.1, f32[2,1,2048]{2,1,0:T(1,128)} %bitcast.2), custom_call_target="tpu_custom_call" | custom-call | tf_op jit(solution)/shard_map/pallas_call | solution.py:508
  109.6 1.6 %copy.9 = f32[8,4096]{1,0:T(8,128)} copy(f32[8,4096]{1,0:T(8,128)} %get-tuple-element.4) | data formatting | bytes 262144
  111.2 2.3 %copy.10 = f32[1080,256]{1,0:T(8,128)} copy(f32[1080,256]{1,0:T(8,128)} %get-tuple-element.5) | data formatting | bytes 2211840

commit v4 on v3

--- a/solution.py
+++ b/solution.py
@@ -42,8 +42,8 @@
     coef_out, res_out,
     xs, tail, rf, rt, rsum, g, gacc, st_loc, st_in, rg_loc, rg_in, fix, mean_own, scale_own, means, mhl,
     cb, stage, oldr, pick, newb, newt,
-    pair_tx, pair_rx, rs_tx, rs_rx, nrm, dmat, c_tx, c_rx, t_buf,
-    x_sem, t_sem, r_sem,
+    pair_tx, pair_rx, rs_tx, rs_rx, nrm, dmat, c_tx, c_rx, t_buf, cout,
+    x_sem, t_sem, r_sem, o_sem,
     st_ss, st_rs, rg_ss, rg_rs, mn_ss, mn_rs, old_ss, old_rs, new_ss, new_rs,
     pr_ss, pr_rs, rs_ss, rs_rs, nm_ss, nm_rs, ag_ss, ag_rs, fw_ss, fw_rs,
     cr_ss, cr_rs, ca_ss, ca_rs,
@@ -97,6 +97,12 @@
         for b in range(2):
             x_copy(b, a).start()
 
+    coef_copy = pltpu.make_async_copy(cout, coef_out, o_sem.at[2])
+
+    def res_copy(h):
+        lanes = pl.ds(h * W, W)
+        return pltpu.make_async_copy(rf.at[pl.ds(0, ROWS), lanes], res_out.at[:, lanes], o_sem.at[h])
+
     barrier = pltpu.get_barrier_semaphore()
 
     @pl.loop(1, NS)
@@ -327,12 +333,15 @@
     def d_view(r, h, core, j):
         return dmat.at[r, pl.ds(al(h * W + core * HW, HW), HW), pl.ds(al(j * W, W), W)]
 
-    def ag_copy(r, h, j, i_src):
-        return rcopy(d_view(r, h, c, i_src), d_view(r, h, c, i_src), ag_ss.at[r, h], ag_rs.at[r, h, i_src],
-                     2 * j + c, v)
-
-    def fw_copy(r, h, j):
-        return rcopy(d_view(r, h, c, j), d_view(r, h, c, j), fw_ss.at[r, h], fw_rs.at[r, h], partner, v)
+    def ag_copy(r, h, j):
+        own = d_view(r, h, c, t)
+        return rcopy(own, own, ag_ss.at[r, h], ag_rs.at[r, h, z], 2 * j + c, v)
+
+    def level(r, h, k):
+        return dmat.at[r, pl.ds(al(h * W + c * HW, HW), HW), pl.ds(al(k * 256, 256), 256)]
+
+    def fw_copy(r, h, k):
+        return rcopy(level(r, h, k), level(r, h, k), fw_ss.at[r, h], fw_rs.at[r, h], partner, v)
 
     def cr_copy(r, h, p):
         return rcopy(c_tx.at[r, h, p], c_rx.at[r, h, v], cr_ss.at[r, h], cr_rs.at[r, h], s, p)
@@ -389,9 +398,8 @@
         for h in range(2):
             @pl.loop(0, NT - 1)
             def _(i):
-                ag_copy(r, h, chip(i), t).start()
-
-            fw_copy(r, h, t).start()
+                ag_copy(r, h, chip(i)).start()
+
 
         if r == 0:
             departed(st_all, st_ss)
@@ -414,11 +422,14 @@
             departed(rs_tx.at[r, h, pl.ds(0, NT - 1)], rs_ss.at[r, h])
 
         for h in range(2):
-            @pl.loop(0, NT - 1)
-            def _(i):
-                j = chip(i)
-                ag_copy(r, h, j, j).wait_recv()
-                fw_copy(r, h, j).start()
+            @pl.loop(0, 7)
+            def _(a):
+                k = (z + zigzag(a, 4)) % 8
+                arrived(level(r, h, k), ag_rs.at[r, h, k])
+                fw_copy(r, h, k).start()
+
+            arrived(d_view(r, h, c, t + 1 - 2 * xh), ag_rs.at[r, h, z])
+            fw_copy(r, h, z).start()
 
             arrived(dmat.at[r, pl.ds(0, HW), :], fw_rs.at[r, h])
 
@@ -480,7 +491,8 @@
             for b in range(2):
                 d0 = colors[0, 0] - b
                 d1 = colors[0, 1] - b
-                coef_out[:, pl.ds(b * BS, BS)] = newt[1 - d1 * d1 + d1 * d1 * d0 * d0 * (2 + b)]
+                cout[:, pl.ds(b * BS, BS)] = newt[1 - d1 * d1 + d1 * d1 * d0 * d0 * (2 + b)]
+            coef_copy.start()
             new_drain(r)
 
         for h in range(2):
@@ -496,10 +508,29 @@
                 transposed(h)
                 gradient(1, h)
             else:
-                res_out[:, lanes] = rf[pl.ds(0, ROWS), lanes]
+                res_copy(h).start()
 
     ca_drain(1, 0)
     ca_drain(1, 1)
+    coef_copy.wait()
+    res_copy(0).wait()
+    res_copy(1).wait()
+
+
+def hand_over(coef, res, coef_out, res_out, coef_vmem, res_vmem, in_sems, out_sems):
+    pieces = [(coef, coef_vmem, coef_out)]
+    for q in range(3):
+        rows = pl.ds(q * 360, 360)
+        pieces.append((res.at[rows, :], res_vmem.at[rows, :], res_out.at[rows, :]))
+    loads = [pltpu.make_async_copy(a, b, in_sems.at[q]) for q, (a, b, _) in enumerate(pieces)]
+    stores = [pltpu.make_async_copy(b, d, out_sems.at[q]) for q, (_, b, d) in enumerate(pieces)]
+    for load in loads:
+        load.start()
+    for load, store in zip(loads, stores):
+        load.wait()
+        store.start()
+    for store in stores:
+        store.wait()
 
 
 def shards(genotypes, residual, coefficients, penalty, colors):
@@ -515,7 +546,7 @@
             pl.BlockSpec(memory_space=pltpu.VMEM),
             pl.BlockSpec(memory_space=pltpu.VMEM),
         ],
-        out_specs=[pl.BlockSpec(memory_space=pltpu.VMEM)] * 2,
+        out_specs=[pl.BlockSpec(memory_space=pl.ANY)] * 2,
         scratch_shapes=[
             vm((2, PAD, BS), BF16), vm((8, 2 * BS), BF16), vm((PAD, K), F32), vm((2, W + 16, PAD), BF16),
             vm((K, W), F32), vm((2, W, BS), F32), vm((W, W), F32),
@@ -528,16 +559,23 @@
             vm((2, 2, NT, HW, W), BF16), vm((2, 2, NT, HW, W), BF16), vm((2, 2, 8, W), F32),
             vm((2, K, BS), BF16),
             vm((2, 2, NV, PR, W), BF16), vm((2, 2, NV, PR, W), BF16), vm((2, 2, NV, PR, W), BF16),
-            dma((2, 8)), dma, dma,
+            vm((8, 2 * BS), F32),
+            dma((2, 8)), dma, dma, dma((3,)),
             dma, dma, dma, dma, dma, dma, dma((2,)), dma((2,)), dma((2,)), dma((2,)),
             dma((2, 2)), dma((2, 2, 8)), dma((2, 2)), dma((2, 2)), dma((2,)), dma((2,)),
-            dma((2, 2)), dma((2, 2, NT)), dma((2, 2)), dma((2, 2)),
+            dma((2, 2)), dma((2, 2, 8)), dma((2, 2)), dma((2, 2)),
             dma((2, 2)), dma((2, 2)), dma((2, 2)), dma((2, 2)),
         ],
         compiler_params=pltpu.CompilerParams(
             collective_id=0, has_side_effects=True, vmem_limit_bytes=56 * 1024 * 1024),
     )(colors.T, genotypes, residual, coefficients, penalty.reshape(2, 1, BS))
-    return (coef, res)
+    return pl.pallas_call(
+        hand_over,
+        out_shape=(jax.ShapeDtypeStruct((8, 2 * BS), F32), jax.ShapeDtypeStruct((ROWS, K), F32)),
+        in_specs=[pl.BlockSpec(memory_space=pl.ANY)] * 2,
+        out_specs=[pl.BlockSpec(memory_space=pl.ANY)] * 2,
+        scratch_shapes=[vm((8, 2 * BS), F32), vm((ROWS, K), F32), dma((4,)), dma((4,))],
+    )(coef, res)
 
 
 def solution(mesh):

time: 114 us -> 111 us (0.974)
  local copies, waits for them, and re-layouts: 3.87 us -> 0 us
    unnamed x2 -> x0, local copies, waits for them, and re-layouts: 3.87 us -> none
    pallas_call x0 -> x1, Pallas kernels: none -> 2.11 us  [shards(): pl.pallas_call(hand_over, out_shape=(jax.ShapeDtypeStruct((8, 2 * BS), F3...]
where the time goes in v4:
time: 111 us
  Pallas kernels  110 us (99%)
    pallas_call x1, Pallas kernels, shards(): pl.pallas_call(kernel, out_shape=(jax.ShapeDtypeStruct((8, 2 * BS), F32),...  108 us

profile of v4, /device:TPU:1, one launch (start us, length us, event | category | flops | bytes accessed | tf_op | source)
XLA Modules:
  0.0 110.8 jit_solution(9699544517163704038)
XLA Ops:
  0.6 108.1 %shard_map.68 = (f32[8,4096]{1,0:T(8,128)}, f32[1080,256]{1,0:T(8,128)}) custom-call(s32[1,2]{1,0:T(1,128)} %bitcast.3, bf16[1080,4096]{1,0:T(8,128)(2,1)} %x_hbm.1, f32[1080,256]{1,0:T(8,128)} %res_hbm.1, f32[8,4096]{1,0:T(8,128)} %coef.1, f32[2,1,2048]{2,1,0:T(1,128)} %bitcast.2), custom_call_target="tpu_custom_call" | custom-call | tf_op jit(solution)/shard_map/pallas_call | solution.py:539
  108.7 2.1 %shard_map.69 = (f32[8,4096]{1,0:T(8,128)}, f32[1080,256]{1,0:T(8,128)}) custom-call(f32[8,4096]{1,0:T(8,128)} %get-tuple-element.4.coef, f32[1080,256]{1,0:T(8,128)} %get-tuple-element.5.res), custom_call_target="tpu_custom_call" | custom-call | tf_op jit(solution)/shard_map/pallas_call | solution.py:572

commit v5 on v4

--- a/solution.py
+++ b/solution.py
@@ -258,14 +258,14 @@
                 rs_copy(r, h, j).start()
 
     def gradient(r, h):
-        @pl.loop(0, 4)
+        @pl.loop(0, 3)
         def _(a):
             product(r, h, a, send=r + h > 0)
 
         if r + h == 0:
             pl.semaphore_wait(barrier, NS - 1 + NV - 1)
 
-            @pl.loop(0, 4)
+            @pl.loop(0, 3)
             def _(a):
                 pair_copy(0, 0, a).start()
 
@@ -276,12 +276,12 @@
             rg_in[s] = rg_loc[...]
             old_sends(0)
 
-        @pl.loop(4, 8)
+        @pl.loop(3, 8)
         def _(a):
             product(r, h, a)
-            send_on(r, h, a - 4)
-
-        @pl.loop(4, 8)
+            send_on(r, h, a - 3)
+
+        @pl.loop(5, 8)
         def _(a):
             send_on(r, h, a)
 

time: 111 us -> 112 us (level)
  no operation moved by 1% of the time
where the time goes in v5:
time: 112 us; the launch traced here: 111 us
  Pallas kernels  111 us (99%)
    pallas_call x1, Pallas kernels, shards(): pl.pallas_call(kernel, out_shape=(jax.ShapeDtypeStruct((8, 2 * BS), F32),...  109 us

profile of v5, /device:TPU:1, one launch (start us, length us, event | category | flops | bytes accessed | tf_op | source)
XLA Modules:
  0.0 111.5 jit_solution(8203581044689313983)
XLA Ops:
  0.6 108.7 %shard_map.68 = (f32[8,4096]{1,0:T(8,128)}, f32[1080,256]{1,0:T(8,128)}) custom-call(s32[1,2]{1,0:T(1,128)} %bitcast.3, bf16[1080,4096]{1,0:T(8,128)(2,1)} %x_hbm.1, f32[1080,256]{1,0:T(8,128)} %res_hbm.1, f32[8,4096]{1,0:T(8,128)} %coef.1, f32[2,1,2048]{2,1,0:T(1,128)} %bitcast.2), custom_call_target="tpu_custom_call" | custom-call | tf_op jit(solution)/shard_map/pallas_call | solution.py:539
  109.3 2.1 %shard_map.69 = (f32[8,4096]{1,0:T(8,128)}, f32[1080,256]{1,0:T(8,128)}) custom-call(f32[8,4096]{1,0:T(8,128)} %get-tuple-element.4.coef, f32[1080,256]{1,0:T(8,128)} %get-tuple-element.5.res), custom_call_target="tpu_custom_call" | custom-call | tf_op jit(solution)/shard_map/pallas_call | solution.py:572
